TPU v7x, 128 devices: a whole 4x4x4 slice. The times are simulated.
128 devices in a mesh: dp: 4 (over z), cols: 32 (over x, y, core).
Axes of the slice: x: 4, y: 4, z: 4, core: 2. Of those that a mesh axis runs over, the one named last changes fastest.
Arguments:
- inputs: bfloat16 [4096, 4096], P('dp', 'cols'), may hold values from -6 to 6
- query_grads: bfloat16 [4096, 8192], P('dp'), may hold values from -0.125 to 0.125, as said below
- momentum: float32 [8192, 4096], P('dp', 'cols'), may hold values from -14 to 14, as said below
Outputs:
- new_momentum: float32 [8192, 4096], P('dp', 'cols')
- update: float32 [8192, 4096], P('dp', 'cols')
Inputs may be any that keep to these rules, and one draw needn't show every extreme that they name: `query_grads`: entries of scale about 4096 ** -0.5. `momentum`: entries of order two.
All inputs are finite; a program needn't handle non-finite values.
Results may differ from a plain program's by a relative error of at most 0.0003.
Values may be sent and summed in bfloat16 or wider, within the bound.
A program may use at most 128 MiB of HBM per device.

v0:
```python
import math

import jax
import jax.numpy as jnp
from jax import lax
from jax.sharding import PartitionSpec as P

D = 4096
HEAD_DIM = 128
NEWTON_STEPS = 5


MOMENTUM_DECAY = 0.95
NORM_EPS = 1e-07
LINEAR_COEF = 3.4445
CUBIC_COEF = -4.775
QUINTIC_COEF = 2.0315
HIGHEST = lax.Precision.HIGHEST
CONTRACT_TOKENS = (((0,), (0,)), ((), ()))


def cut_along(value, dim, length):
    shape = value.shape
    blocks = value.reshape(*shape[:dim], length, shape[dim] // length, *shape[dim + 1 :])
    return jnp.moveaxis(blocks, dim, 0)


def summed_on_arrival(value, axis, dim):
    blocks = cut_along(value, dim, lax.axis_size(axis))
    arrived = lax.all_to_all(blocks, axis, split_axis=0, concat_axis=0, tiled=True)
    return arrived.sum(axis=0)


def sent_to_all(value, axis):
    length = lax.axis_size(axis)
    return lax.all_to_all(
        jnp.broadcast_to(value[None], (length, *value.shape)), axis, 0, 0, tiled=True
    )


def in_order(blocks, dim):
    shape = list(blocks.shape[1:])
    shape[dim] *= blocks.shape[0]
    return jnp.moveaxis(blocks, 0, dim).reshape(shape)


def gathered_copies(value, axis, dim):
    blocks = sent_to_all(value, axis)
    return in_order(blocks, dim)


def polynomial(gram_matrix):
    matrix_order = gram_matrix.shape[-1]
    trace_sum = jnp.sum(jnp.diagonal(gram_matrix, axis1=1, axis2=2), axis=1)
    norm_scale = jnp.sqrt(trace_sum) + NORM_EPS
    current = gram_matrix / (norm_scale * norm_scale)[:, None, None]
    identity = jnp.eye(matrix_order, dtype=jnp.float32)
    factor = jnp.broadcast_to(identity, gram_matrix.shape)
    for sweep_index in range(NEWTON_STEPS):
        square = jnp.einsum("hij,hjk->hik", current, current, precision=HIGHEST)
        poly_term = LINEAR_COEF * identity + CUBIC_COEF * current + QUINTIC_COEF * square
        factor = jnp.einsum("hij,hjk->hik", poly_term, factor, precision=HIGHEST)
        if sweep_index + 1 < NEWTON_STEPS:
            inner = jnp.einsum("hij,hjk->hik", current, poly_term, precision=HIGHEST)
            current = jnp.einsum("hij,hjk->hik", poly_term, inner, precision=HIGHEST)
    return factor / norm_scale[:, None, None]


def shards(inputs, query_grads, momentum):
    row_count = momentum.shape[0]
    col_count = momentum.shape[1]
    gradient = summed_on_arrival(
        lax.dot_general(query_grads, inputs, CONTRACT_TOKENS, preferred_element_type=jnp.float32),
        "dp",
        0,
    )
    new_momentum = MOMENTUM_DECAY * momentum + gradient
    local_heads = row_count // HEAD_DIM
    blocks = new_momentum.reshape(local_heads, HEAD_DIM, col_count)
    partial_value = jnp.einsum("hik,hjk->hij", blocks, blocks, precision=HIGHEST)
    owners = lax.axis_size("cols")
    slot_count = -(-local_heads // owners)
    padded = jnp.pad(partial_value, ((0, slot_count * owners - local_heads), (0, 0), (0, 0)))
    owned_gram = summed_on_arrival(
        padded.reshape(slot_count, owners, HEAD_DIM, HEAD_DIM), "cols", 1
    )
    owned_factor = polynomial(owned_gram.reshape(slot_count, HEAD_DIM, HEAD_DIM))
    returned = gathered_copies(owned_factor.reshape(slot_count, 1, HEAD_DIM, HEAD_DIM), "cols", 1)
    factor = returned.reshape(slot_count * owners, HEAD_DIM, HEAD_DIM)[:local_heads]
    update = math.sqrt(D) * jnp.einsum("hij,hjk->hik", factor, blocks, precision=HIGHEST)
    return (new_momentum, update.reshape(row_count, col_count))


def solution(mesh):
    placed = (P("dp", "cols"), P("dp", None), P("dp", "cols"))
    return jax.shard_map(
        shards,
        mesh=mesh,
        in_specs=placed,
        out_specs=(P("dp", "cols"), P("dp", "cols")),
        check_vma=False,
    )
```

profile of v0, /device:TPU:1, one launch (start us, length us, event | category | flops | bytes accessed | tf_op | source)
XLA Modules:
  0.0 148.0 jit_solution(14572971154629413474)
XLA Ops:
  0.6 0.9 copy-done
  1.6 8.2 %fusion.7 = f32[8192,128]{1,0:T(8,128)S(1)} fusion(bf16[1024,8192]{1,0:T(8,128)(2,1)} %param.4, bf16[1024,128]{1,0:T(8,128)(2,1)S(1)} %copy-done), kind=kOutput, calls=%fused_computation.26 | convolution fusion | flops 2147483648 | bytes 21233664 | tf_op jit(solution)/shard_map/dot_general | solution.py:73
  9.8 53.7 %all_to_all.15 = f32[4,2048,128]{2,1,0:T(8,128)} all-to-all(f32[4,2048,128]{2,1,0:T(8,128)S(1)} %bitcast.50), channel_id=1, replica_groups=mesh['dp'=4,'cols'=32] {'dp'}, dimensions={0} | all-to-all | bytes 8388608 | tf_op jit(solution)/shard_map/all_to_all | solution.py:30
  63.5 2.6 %reduce_sum.27 = f32[2048,128]{1,0:T(8,128)S(1)} reduce(f32[4,2048,128]{2,1,0:T(8,128)} %all_to_all.15, f32[]{:T(128)} %constant.8.clone.1), dimensions={0}, to_apply=%region_0.0 | reduce | flops 786432 | bytes 5242884 | tf_op jit(solution)/shard_map/reduce_sum | solution.py:31
  66.3 2.3 %fusion.8 = f32[16,128,128]{2,1,0:T(8,128)S(1)} fusion(f32[16,128,128]{2,1,0:T(8,128)S(1)} %bitcast.51), kind=kOutput, calls=%fused_computation.27 | convolution fusion | flops 402653184 | bytes 2097152 | tf_op jit(solution)/shard_map/hik,hjk->hij/dot_general | solution.py:80
  68.6 1.6 %pad_bitcast_fusion = f32[32,1,1,128,128]{4,3,2,1,0:T(8,128)} fusion(f32[16,128,128]{2,1,0:T(8,128)S(1)} %fusion.8), kind=kLoop, calls=%fused_computation.1 | loop fusion | bytes 3145728 | tf_op jit(solution)/shard_map/transpose;reshape;reshape | solution.py:25
  70.2 8.9 %all-to-all-start.1 = ((f32[32,1,1,128,128]{4,3,2,1,0:T(8,128)}), f32[32,1,1,128,128]{4,3,2,1,0:T(8,128)S(1)}, u32[]{:S(2)}, u32[]{:S(2)}) async-start(f32[32,1,1,128,128]{4,3,2,1,0:T(8,128)} %pad_bitcast_fusion), calls=%async_computation.1 | async-start | bytes 4194304 | tf_op jit(solution)/shard_map/all_to_all | solution.py:30
  79.1 28.3 %all-to-all-done.1 = f32[32,1,1,128,128]{4,3,2,1,0:T(8,128)S(1)} async-done(((f32[32,1,1,128,128]{4,3,2,1,0:T(8,128)}), f32[32,1,1,128,128]{4,3,2,1,0:T(8,128)S(1)}, u32[]{:S(2)}, u32[]{:S(2)}) %all-to-all-start.1) | async-done | bytes 2097184 | tf_op jit(solution)/shard_map/all_to_all | solution.py:30
  107.5 1.2 gather_fusion
  108.8 0.6 reduce.2
  110.1 0.2 fusion.4
  110.3 0.2 fusion.6
  110.7 0.2 fusion.9
  110.9 0.2 fusion.3
  111.8 0.2 fusion.2
  112.6 0.2 fusion.1
  112.8 0.2 fusion.14
  113.0 0.2 fusion.18
  113.2 0.2 fusion.15
  113.4 0.2 fusion
  113.7 0.2 convolution_divide_fusion
  113.9 0.2 broadcast_in_dim.6
  114.1 31.8 %all_to_all.16 = f32[32,1,1,128,128]{4,3,2,1,0:T(8,128)S(1)} all-to-all(f32[32,1,1,128,128]{4,3,2,1,0:T(8,128)S(1)} %broadcast_in_dim.6), channel_id=1, replica_groups=mesh['dp'=4,'cols'=32] {'cols'}, dimensions={0} | all-to-all | bytes 4194304 | tf_op jit(solution)/shard_map/all_to_all | solution.py:36
  145.9 2.1 %convolution_multiply_fusion = f32[16,128,128]{2,1,0:T(8,128)} fusion(f32[16,128,128]{2,1,0:T(8,128)S(1)} %bitcast.52, f32[32,1,1,128,128]{4,3,0,2,1:T(8,128)S(1)} %bitcast.53), kind=kOutput, calls=%fused_computation.2 | convolution fusion | flops 402915328 | bytes 3145728 | tf_op jit(solution)/shard_map/hij,hjk->hik/dot_general | solution.py:90
  (15 shorter events, 1.7 us)
Async XLA Ops:
  0.6 1.0 copy-start
  63.5 2.6 %copy-start.2 = (f32[2048,128]{1,0:T(8,128)S(1)}, f32[2048,128]{1,0:T(8,128)}, u32[]{:S(2)}) copy-start(f32[2048,128]{1,0:T(8,128)} %param.5) | copy-start | bytes 3145732
  66.3 79.6 %copy-start.1 = (f32[2048,128]{1,0:T(8,128)}, f32[2048,128]{1,0:T(8,128)S(1)}, u32[]{:S(2)}) copy-start(f32[2048,128]{1,0:T(8,128)S(1)} %multiply_add_fusion) | copy-start | bytes 3145732
  70.2 37.2 %all-to-all-start.1 = ((f32[32,1,1,128,128]{4,3,2,1,0:T(8,128)}), f32[32,1,1,128,128]{4,3,2,1,0:T(8,128)S(1)}, u32[]{:S(2)}, u32[]{:S(2)}) async-start(f32[32,1,1,128,128]{4,3,2,1,0:T(8,128)} %pad_bitcast_fusion), calls=%async_computation.1 | async-start | bytes 4194304 | tf_op jit(solution)/shard_map/all_to_all | solution.py:30
where the time goes:
time: 148 us
  blocking collectives  85.5 us (58%)
  waiting for transfers between devices  28.3 us (19%)
  matrix products  16.3 us (11%)
  starting transfers between devices  8.9 us (6%)
  local copies, waits for them, and re-layouts  4.02 us (3%)
  other arithmetic  3.44 us (2%)
  between operations  1.55 us (1%)
    all_to_all x1, blocking collectives, summed_on_arrival(): lax.all_to_all(blocks, axis, split_axis=0, concat_axis=0, tiled=True)  53.7 us
    all_to_all x1, blocking collectives, sent_to_all(): lax.all_to_all(jnp.broadcast_to(value[None], (length, *value.shape)), axi...  31.8 us
    all_to_all x1, waiting for transfers between devices, summed_on_arrival(): lax.all_to_all(blocks, axis, split_axis=0, concat_axis=0, tiled=True)  28.3 us
    all_to_all x1, starting transfers between devices, summed_on_arrival(): lax.all_to_all(blocks, axis, split_axis=0, concat_axis=0, tiled=True)  8.9 us
    dot_general x1, matrix products, shards(): lax.dot_general(query_grads, inputs, CONTRACT_TOKENS, preferred_element_t...  8.24 us
  transfers between devices with their start and end apart: 1, of which 1 were waited for; matrix products, arithmetic and copies ran while one was open for 0% of the time, Pallas kernels for 0%

commit v1 on v0

v1 whole, which is shorter than its diff:
```python
import functools
import math

import jax
import jax.numpy as jnp
from jax import lax
from jax.experimental import pallas as pl
from jax.experimental.pallas import tpu as pltpu
from jax.sharding import PartitionSpec as P

HEAD = 128
STEPS = 5
MOMENTUM_DECAY = 0.95
NORM_EPS = 1e-07
C1 = 3.4445
C3 = -4.775
C5 = 2.0315
MESH = pl.DeviceIdType.MESH
F32 = jnp.float32
BF16 = jnp.bfloat16

GRAD_CODE = (0.125, 2.0**-6, 4)
GRAM_CODE = (8.0, 2.0**-12, 3)
ROOT_CODE = (0.0625, 2.0**-6, 4)
RELAY_A, RELAY_B, DIRECT_B, DIRECT_A, SUM_A, SUM_B = range(6)


def encode(value, code):
    a, s, doublings = code
    grown = jnp.abs(value) * (s / a) + s
    for _ in range(doublings):
        grown = grown * grown
    return jnp.where(value < 0.0, -grown, grown).astype(BF16)


def decode(sent, code):
    a, s, doublings = code
    wide = sent.astype(F32)
    grown = jnp.exp(jnp.log(jnp.abs(wide)) * (0.5**doublings))
    size = grown * (a / s) - a
    return jnp.where(wide < 0.0, -size, size)


def split(value):
    high = value.astype(BF16)
    low = (value - high.astype(F32)).astype(BF16)
    return high, low


def dot_nn(a, b):
    return lax.dot_general(a, b, (((1,), (0,)), ((), ())), preferred_element_type=F32)


def dot_nt(a, b):
    return lax.dot_general(a, b, (((1,), (1,)), ((), ())), preferred_element_type=F32)


def mul3(a, b):
    ah, al = a
    bh, bl = b
    return dot_nn(ah, bh) + (dot_nn(ah, bl) + dot_nn(al, bh))


def kernel(
    dims,
    x_hbm,
    q_hbm,
    m_hbm,
    nm_ref,
    up_ref,
    x_ref,
    xt_ref,
    q_ref,
    m_ref,
    own_ref,
    zsend,
    zrecv,
    gsend,
    grecv,
    gown,
    fsend,
    frecv,
    x_sem,
    m_sem,
    q_sem,
    zsend_sem,
    zrecv_sem,
    gsend_sem,
    grecv_sem,
    fsend_sem,
    frecv_sem,
):
    cols, heads, chunks, width = dims
    half_rows = chunks * width
    rows = 2 * half_rows
    per_chunk = width // HEAD
    half_heads = heads // 2

    z = lax.axis_index("dp")
    c = lax.axis_index("cols")
    right = lax.rem(z + 1, 4)
    left = lax.rem(z + 3, 4)
    opposite = lax.rem(z + 2, 4)

    own_head = c // 2
    is_owner = jnp.logical_and(own_head < heads, lax.rem(c, 2) == lax.rem(own_head, 2))
    own_chunk = lax.rem(own_head, half_heads) // per_chunk

    def owner_of(head):
        return 2 * head + lax.rem(head, 2)

    row = lax.broadcasted_iota(jnp.int32, (HEAD, HEAD), 0)
    column = lax.broadcasted_iota(jnp.int32, (HEAD, HEAD), 1)
    identity = jnp.where(row == column, 1.0, 0.0)

    x_copy = pltpu.make_async_copy(x_hbm, x_ref, x_sem)
    x_copy.start()

    def q_copy(slot, target, half, k):
        start = pl.multiple_of(target * rows + half * half_rows + k * width, width)
        return pltpu.make_async_copy(q_hbm.at[:, pl.ds(start, width)], q_ref.at[slot], q_sem.at[slot])

    for k in range(chunks):
        q_copy(2 * k, opposite, 0, k).start()
        q_copy(2 * k + 1, opposite, 1, k).start()
    second = 2 * chunks
    for k in range(chunks):
        q_copy(second + 4 * k, right, 1, k).start()
        q_copy(second + 4 * k + 1, left, 0, k).start()
        q_copy(second + 4 * k + 2, right, 0, k).start()
        q_copy(second + 4 * k + 3, left, 1, k).start()
    third = 6 * chunks
    m_copy = pltpu.make_async_copy(m_hbm, m_ref, m_sem)
    for k in range(chunks):
        q_copy(third + 2 * k, z, 0, k).start()
        q_copy(third + 2 * k + 1, z, 1, k).start()
    m_copy.start()

    barrier = pltpu.get_barrier_semaphore()
    for step in (1, 3):
        pl.semaphore_signal(barrier, inc=1, device_id={"dp": lax.rem(z + step, 4)}, device_id_type=MESH)

    def greet(step, carry):
        pl.semaphore_signal(barrier, inc=1, device_id={"cols": lax.rem(c + step, cols)}, device_id_type=MESH)
        return carry

    lax.fori_loop(1, cols, greet, 0)

    x_copy.wait()
    xt_ref[...] = x_ref[...].T
    pl.semaphore_wait(barrier, cols - 1 + 2)

    def product(slot):
        pltpu.make_async_copy(q_hbm.at[:, pl.ds(0, width)], q_ref.at[slot], q_sem.at[slot]).wait()
        return dot_nn(xt_ref[...], q_ref[slot])

    def z_copy(message, k, target):
        return pltpu.make_async_remote_copy(
            src_ref=zsend.at[message, k],
            dst_ref=zrecv.at[message, k],
            send_sem=zsend_sem.at[message, k],
            recv_sem=zrecv_sem.at[message, k],
            device_id={"dp": target},
            device_id_type=MESH,
        )

    def z_send(message, k, target, value):
        zsend[message, k] = encode(value, GRAD_CODE)
        z_copy(message, k, target).start()

    def z_arrived(message, k):
        z_copy(message, k, right).wait_recv()
        return decode(zrecv[message, k], GRAD_CODE)

    def relay(k, carry):
        z_send(RELAY_A, k, right, product(2 * k))
        z_send(RELAY_B, k, left, product(2 * k + 1))
        return carry

    lax.fori_loop(0, chunks, relay, 0)

    def onward(k, carry):
        z_send(DIRECT_B, k, right, product(second + 4 * k))
        z_send(DIRECT_A, k, left, product(second + 4 * k + 1))
        mine = product(second + 4 * k + 2)
        z_send(SUM_A, k, right, mine + z_arrived(RELAY_A, k))
        mine = product(second + 4 * k + 3)
        z_send(SUM_B, k, left, mine + z_arrived(RELAY_B, k))
        return carry

    lax.fori_loop(0, chunks, onward, 0)

    def kept(k, carry):
        own_ref[2 * k] = product(third + 2 * k)
        own_ref[2 * k + 1] = product(third + 2 * k + 1)
        return carry

    lax.fori_loop(0, chunks, kept, 0)
    m_copy.wait()

    def g_copy(head):
        owner = owner_of(head)
        slot = jnp.maximum(lax.rem(c - owner + cols, cols) - 1, 0)
        return pltpu.make_async_remote_copy(
            src_ref=gsend.at[head],
            dst_ref=grecv.at[slot],
            send_sem=gsend_sem.at[head],
            recv_sem=grecv_sem.at[slot],
            device_id={"cols": owner},
            device_id_type=MESH,
        )

    def head_done(head, total):
        start = pl.multiple_of(head * HEAD, HEAD)
        block = m_ref[pl.ds(start, HEAD), :] * MOMENTUM_DECAY + total.T
        nm_ref[pl.ds(start, HEAD), :] = block
        high, low = split(block)
        cross = dot_nt(high, low)
        gram = dot_nt(high, high) + (cross + dot_nt(low, high))

        @pl.when(c == owner_of(head))
        def _():
            gown[...] = gram

        @pl.when(c != owner_of(head))
        def _():
            gsend[head] = encode(gram, GRAM_CODE)
            g_copy(head).start()

    def f_copy(step):
        return pltpu.make_async_remote_copy(
            src_ref=fsend,
            dst_ref=frecv.at[own_head],
            send_sem=fsend_sem.at[step],
            recv_sem=frecv_sem.at[own_head],
            device_id={"cols": lax.rem(c + step, cols)},
            device_id_type=MESH,
        )

    def own_polynomial():
        def add(slot, total):
            pltpu.make_async_remote_copy(
                src_ref=gsend.at[0],
                dst_ref=grecv.at[slot],
                send_sem=gsend_sem.at[0],
                recv_sem=grecv_sem.at[slot],
                device_id={"cols": lax.rem(c + 1, cols)},
                device_id_type=MESH,
            ).wait_recv()
            return total + decode(grecv[slot], GRAM_CODE)

        gram = lax.fori_loop(0, cols - 1, add, gown[...])
        trace = jnp.sum(jnp.sum(gram * identity, axis=0, keepdims=True), axis=1, keepdims=True)
        norm = jnp.sqrt(trace) + NORM_EPS
        current = gram / (norm * norm)
        factor = None
        for sweep in range(STEPS):
            parts = split(current)
            square = mul3(parts, parts)
            poly = C1 * identity + C3 * current + C5 * square
            poly_parts = split(poly)
            factor = poly if factor is None else mul3(poly_parts, split(factor))
            if sweep + 1 < STEPS:
                inner = mul3(parts, poly_parts)
                current = mul3(poly_parts, split(inner))
        mean = jnp.sum(jnp.sum(factor * identity, axis=0, keepdims=True), axis=1, keepdims=True) * (1.0 / HEAD)
        fsend[pl.ds(0, HEAD), :] = encode(factor - mean * identity, ROOT_CODE)
        which = lax.broadcasted_iota(jnp.int32, (16, HEAD), 0)
        pieces = jnp.zeros((16, HEAD), F32)
        for row_index, rest in ((0, norm), (3, mean)):
            rest = jnp.broadcast_to(rest, (16, HEAD))
            for piece in range(3):
                part = rest.astype(BF16).astype(F32)
                pieces = jnp.where(which == row_index + piece, part, pieces)
                rest = rest - part
        fsend[pl.ds(HEAD, 16), :] = pieces.astype(BF16)

        def send(step, carry):
            f_copy(step).start()
            return carry

        lax.fori_loop(1, cols, send, 0)

    def finish(k, carry):
        @pl.when(k < chunks)
        def _():
            total = own_ref[2 * k] + (z_arrived(DIRECT_A, k) + z_arrived(SUM_A, k))
            for j in range(per_chunk):
                head_done(k * per_chunk + j, total[:, j * HEAD : (j + 1) * HEAD])
            total = own_ref[2 * k + 1] + (z_arrived(DIRECT_B, k) + z_arrived(SUM_B, k))
            for j in range(per_chunk):
                head_done(half_heads + k * per_chunk + j, total[:, j * HEAD : (j + 1) * HEAD])

        @pl.when(jnp.logical_and(is_owner, own_chunk == k - 1))
        def _():
            own_polynomial()

        return carry

    lax.fori_loop(0, chunks + 1, finish, 0)

    def apply(index, carry):
        k = index // (2 * per_chunk)
        j = lax.rem(index, 2 * per_chunk)
        head = (j // per_chunk) * half_heads + k * per_chunk + lax.rem(j, per_chunk)
        mine = c == owner_of(head)

        @pl.when(jnp.logical_not(mine))
        def _():
            pltpu.make_async_remote_copy(
                src_ref=fsend,
                dst_ref=frecv.at[head],
                send_sem=fsend_sem.at[0],
                recv_sem=frecv_sem.at[head],
                device_id={"cols": lax.rem(c + 1, cols)},
                device_id_type=MESH,
            ).wait_recv()

        @pl.when(mine)
        def _():
            frecv[head] = fsend[...]

        pieces = frecv[head, pl.ds(HEAD, 16), :].astype(F32)
        norm = pieces[0:1, :] + (pieces[1:2, :] + pieces[2:3, :])
        mean = pieces[3:4, :] + (pieces[4:5, :] + pieces[5:6, :])
        factor = decode(frecv[head, pl.ds(0, HEAD), :], ROOT_CODE) + mean * identity
        scale = math.sqrt(cols * HEAD) / norm
        start = pl.multiple_of(head * HEAD, HEAD)
        block = nm_ref[pl.ds(start, HEAD), :]
        up_ref[pl.ds(start, HEAD), :] = mul3(split(factor), split(block)) * scale
        return carry

    lax.fori_loop(0, heads, apply, 0)

    def z_drain(k, carry):
        for message in range(6):
            z_copy(message, k, right).wait_send()
        return carry

    lax.fori_loop(0, chunks, z_drain, 0)

    def g_drain(head, carry):
        @pl.when(c != owner_of(head))
        def _():
            g_copy(head).wait_send()

        return carry

    lax.fori_loop(0, heads, g_drain, 0)

    @pl.when(is_owner)
    def _():
        def f_drain(step, carry):
            f_copy(step).wait_send()
            return carry

        lax.fori_loop(1, cols, f_drain, 0)


def shards(cols, chunks, inputs, query_grads, momentum):
    rows = momentum.shape[0]
    heads = rows // HEAD
    width = rows // (2 * chunks)
    tokens = inputs.shape[0]
    dims = (cols, heads, chunks, width)
    out = jax.ShapeDtypeStruct((rows, HEAD), F32)
    return pl.pallas_call(
        functools.partial(kernel, dims),
        out_shape=(out, out),
        in_specs=[pl.BlockSpec(memory_space=pl.ANY)] * 3,
        out_specs=(pl.BlockSpec(memory_space=pltpu.VMEM),) * 2,
        scratch_shapes=[
            pltpu.VMEM((tokens, HEAD), BF16),
            pltpu.VMEM((HEAD, tokens), BF16),
            pltpu.VMEM((8 * chunks, tokens, width), BF16),
            pltpu.VMEM((rows, HEAD), F32),
            pltpu.VMEM((2 * chunks, HEAD, width), F32),
            pltpu.VMEM((6, chunks, HEAD, width), BF16),
            pltpu.VMEM((6, chunks, HEAD, width), BF16),
            pltpu.VMEM((heads, HEAD, HEAD), BF16),
            pltpu.VMEM((cols - 1, HEAD, HEAD), BF16),
            pltpu.VMEM((HEAD, HEAD), F32),
            pltpu.VMEM((HEAD + 16, HEAD), BF16),
            pltpu.VMEM((heads, HEAD + 16, HEAD), BF16),
            pltpu.SemaphoreType.DMA,
            pltpu.SemaphoreType.DMA,
            pltpu.SemaphoreType.DMA((8 * chunks,)),
            pltpu.SemaphoreType.DMA((6, chunks)),
            pltpu.SemaphoreType.DMA((6, chunks)),
            pltpu.SemaphoreType.DMA((heads,)),
            pltpu.SemaphoreType.DMA((cols - 1,)),
            pltpu.SemaphoreType.DMA((cols,)),
            pltpu.SemaphoreType.DMA((heads,)),
        ],
        compiler_params=pltpu.CompilerParams(collective_id=0, has_side_effects=True),
    )(inputs, query_grads, momentum)


def solution(mesh):
    placed = (P("dp", "cols"), P("dp", None), P("dp", "cols"))
    return jax.shard_map(
        functools.partial(shards, mesh.shape["cols"], 4),
        mesh=mesh,
        in_specs=placed,
        out_specs=(P("dp", "cols"), P("dp", "cols")),
        check_vma=False,
    )
```

time: 148 us -> 66.1 us (0.45)
  blocking collectives: 85.5 us -> 0 us
  Pallas kernels: 0 us -> 60.7 us
  waiting for transfers between devices: 28.3 us -> 0 us
  matrix products: 16.3 us -> 0 us
  starting transfers between devices: 8.9 us -> 0 us
  other arithmetic: 3.44 us -> 0 us
    all_to_all x2 -> x0, blocking collectives: 85.5 us -> none  [the longest x1 53.7 us: summed_on_arrival(): lax.all_to_all(blocks, axis, split_axis=0, concat_axis=0, tiled=True)]
    pallas_call x0 -> x1, Pallas kernels: none -> 60.7 us  [shards(): pl.pallas_call(functools.partial(kernel, dims), out_shape=(out, out), in_...]
    all_to_all x1 -> x0, waiting for transfers between devices: 28.3 us -> none  [summed_on_arrival(): lax.all_to_all(blocks, axis, split_axis=0, concat_axis=0, tiled=True)]
    dot_general x21 -> x0, matrix products: 16.3 us -> none  [the longest x1 8.24 us: shards(): lax.dot_general(query_grads, inputs, CONTRACT_TOKENS, preferred_element_t...]
    all_to_all x1 -> x0, starting transfers between devices: 8.9 us -> none  [summed_on_arrival(): lax.all_to_all(blocks, axis, split_axis=0, concat_axis=0, tiled=True)]
    unnamed x6 -> x2, local copies, waits for them, and re-layouts: 0.96 us -> 4.52 us
    reduce_sum x3 -> x0, other arithmetic: 3.31 us -> none  [the longest x2 2.71 us: summed_on_arrival(): return arrived.sum(axis=0)]
    another operation x1 -> x0, local copies, waits for them, and re-layouts: 1.59 us -> none  [cut_along(): return jnp.moveaxis(blocks, dim, 0)]
  transfers between devices with their start and end apart: 1 -> 0, of which waited for: 1 -> 0; matrix products, arithmetic and copies ran while one was open for 0% -> 0% of each run, Pallas kernels for 0% -> 0%
where the time goes in v1:
time: 66.1 us; the launch traced here: 65.9 us
  Pallas kernels  60.7 us (92%)
  local copies, waits for them, and re-layouts  4.52 us (7%)
    pallas_call x1, Pallas kernels, shards(): pl.pallas_call(functools.partial(kernel, dims), out_shape=(out, out), in_...  60.7 us
    unnamed x2, local copies, waits for them, and re-layouts  4.52 us

profile of v1, /device:TPU:1, one launch (start us, length us, event | category | flops | bytes accessed | tf_op | source)
XLA Modules:
  0.0 65.9 jit_solution(18051268486290046862)
XLA Ops:
  0.6 60.7 %shard_map.50 = (f32[2048,128]{1,0:T(8,128)}, f32[2048,128]{1,0:T(8,128)}) custom-call(bf16[1024,128]{1,0:T(8,128)(2,1)} %x_hbm.1, bf16[1024,8192]{1,0:T(8,128)(2,1)} %q_hbm.1, f32[2048,128]{1,0:T(8,128)} %m_hbm.1), custom_call_target="tpu_custom_call" | custom-call | tf_op jit(solution)/shard_map/pallas_call | solution.py:367
  61.4 2.3 %copy.7 = f32[2048,128]{1,0:T(8,128)} copy(f32[2048,128]{1,0:T(8,128)} %get-tuple-element.4) | data formatting | bytes 2097152
  63.6 2.3 %copy.8 = f32[2048,128]{1,0:T(8,128)} copy(f32[2048,128]{1,0:T(8,128)} %get-tuple-element.5) | data formatting | bytes 2097152

commit v2 on v1

v2 whole, which is shorter than its diff:
```python
import functools
import math

import jax
import jax.numpy as jnp
from jax import lax
from jax.experimental import pallas as pl
from jax.experimental.pallas import tpu as pltpu
from jax.sharding import PartitionSpec as P

HEAD = 128
HALF = HEAD // 2
STEPS = 5
MOMENTUM_DECAY = 0.95
NORM_EPS = 1e-07
C1 = 3.4445
C3 = -4.775
C5 = 2.0315
MESH = pl.DeviceIdType.MESH
F32 = jnp.float32
BF16 = jnp.bfloat16

GRAD_CODE = (0.125, 2.0**-6, 4)
GRAM_CODE = (8.0, 2.0**-12, 3)
ROOT_CODE = (0.0625, 2.0**-6, 4)
RELAY_A, RELAY_B, DIRECT_B, DIRECT_A, SUM_A, SUM_B = range(6)


def encode(value, code):
    a, s, doublings = code
    grown = jnp.abs(value) * (s / a) + s
    for _ in range(doublings):
        grown = grown * grown
    return jnp.where(value < 0.0, -grown, grown).astype(BF16)


def decode(sent, code):
    a, s, doublings = code
    wide = sent.astype(F32)
    grown = jnp.exp(jnp.log(jnp.abs(wide)) * (0.5**doublings))
    size = grown * (a / s) - a
    return jnp.where(wide < 0.0, -size, size)


def split(value):
    high = value.astype(BF16)
    low = (value - high.astype(F32)).astype(BF16)
    return high, low


def dot_nn(a, b):
    return lax.dot_general(a, b, (((1,), (0,)), ((), ())), preferred_element_type=F32)


def dot_nt(a, b):
    return lax.dot_general(a, b, (((1,), (1,)), ((), ())), preferred_element_type=F32)


def mul3(a, b):
    ah, al = a
    bh, bl = b
    return dot_nn(ah, bh) + (dot_nn(ah, bl) + dot_nn(al, bh))


def iotas(rows):
    return (
        lax.broadcasted_iota(jnp.int32, (rows, HEAD), 0),
        lax.broadcasted_iota(jnp.int32, (rows, HEAD), 1),
    )


def pack(matrix):
    row, lane = iotas(HALF)
    return jnp.where(lane > row, matrix[:HALF], pltpu.roll(matrix[HALF:], HALF, 1))


def unpack(packed):
    row, lane = iotas(HALF)
    top = jnp.where(lane > row, packed, 0.0)
    bottom = pltpu.roll(jnp.where(lane < row, packed, 0.0), HALF, 1)
    half = jnp.concatenate([top, bottom], axis=0)
    return half + half.T


def kernel(
    dims,
    x_hbm,
    q_hbm,
    m_hbm,
    nm_ref,
    up_ref,
    x_ref,
    xt_ref,
    q_ref,
    m_ref,
    own_ref,
    zsend,
    zrecv,
    gsend,
    grecv,
    fsend,
    frecv,
    x_sem,
    m_sem,
    q_sem,
    zsend_sem,
    zrecv_sem,
    gsend_sem,
    grecv_sem,
    fsend_sem,
    frecv_sem,
):
    cols, heads, chunks, width = dims
    half_rows = chunks * width
    rows = 2 * half_rows
    per_chunk = width // HEAD
    half_heads = heads // 2
    groups = 2
    wide = half_rows // groups
    per_group = chunks // groups

    z = lax.axis_index("dp")
    c = lax.axis_index("cols")
    right = lax.rem(z + 1, 4)
    left = lax.rem(z + 3, 4)
    opposite = lax.rem(z + 2, 4)

    own_head = c // 2
    is_owner = jnp.logical_and(own_head < heads, lax.rem(c, 2) == lax.rem(own_head, 2))

    row, lane = iotas(HEAD)
    identity = jnp.where(row == lane, 1.0, 0.0)
    which = iotas(16)[0]

    def owner_of(head):
        return 2 * head + lax.rem(head, 2)

    x_copy = pltpu.make_async_copy(x_hbm, x_ref, x_sem)
    x_copy.start()

    def q_copy(slot, target, half, g):
        start = pl.multiple_of(target * rows + half * half_rows + g * wide, wide)
        return pltpu.make_async_copy(q_hbm.at[:, pl.ds(start, wide)], q_ref.at[slot], q_sem.at[slot])

    for g in range(groups):
        q_copy(2 * g, opposite, 0, g).start()
        q_copy(2 * g + 1, opposite, 1, g).start()
    q_copy(4, right, 1, 0).start()
    q_copy(5, left, 0, 0).start()
    for g in range(groups):
        q_copy(8 + 2 * g, z, 0, g).start()
        q_copy(9 + 2 * g, z, 1, g).start()
    q_copy(12, right, 0, 0).start()
    q_copy(13, left, 1, 0).start()
    q_copy(6, right, 1, 1).start()
    q_copy(7, left, 0, 1).start()
    q_copy(14, right, 0, 1).start()
    q_copy(15, left, 1, 1).start()
    m_copy = pltpu.make_async_copy(m_hbm, m_ref, m_sem)
    m_copy.start()

    barrier = pltpu.get_barrier_semaphore()
    for step in (1, 3):
        pl.semaphore_signal(barrier, inc=1, device_id={"dp": lax.rem(z + step, 4)}, device_id_type=MESH)

    def greet(step, carry):
        pl.semaphore_signal(barrier, inc=1, device_id={"cols": lax.rem(c + step, cols)}, device_id_type=MESH)
        return carry

    lax.fori_loop(1, cols, greet, 0)

    x_copy.wait()
    xt_ref[...] = x_ref[...].T

    def q_wait(slot):
        pltpu.make_async_copy(q_hbm.at[:, pl.ds(0, wide)], q_ref.at[slot], q_sem.at[slot]).wait()

    def product(slot):
        return dot_nn(xt_ref[...], q_ref[slot])

    def z_copy(message, k, target):
        return pltpu.make_async_remote_copy(
            src_ref=zsend.at[message, k],
            dst_ref=zrecv.at[message, k],
            send_sem=zsend_sem.at[message, k],
            recv_sem=zrecv_sem.at[message, k],
            device_id={"dp": target},
            device_id_type=MESH,
        )

    def z_store(message, g, value):
        for i in range(per_group):
            zsend[message, g * per_group + i] = encode(value[:, i * width : (i + 1) * width], GRAD_CODE)

    def z_start(message, g, target):
        for i in range(per_group):
            z_copy(message, g * per_group + i, target).start()

    def z_wait(message, k):
        z_copy(message, k, right).wait_recv()

    def z_value(message, k):
        return decode(zrecv[message, k], GRAD_CODE)

    for g in range(groups):
        q_wait(2 * g)
        q_wait(2 * g + 1)
        z_store(RELAY_A, g, product(2 * g))
        z_store(RELAY_B, g, product(2 * g + 1))
        if g == 0:
            pl.semaphore_wait(barrier, cols - 1 + 2)
        z_start(RELAY_A, g, right)
        z_start(RELAY_B, g, left)

    def direct(g):
        q_wait(4 + 2 * g)
        q_wait(5 + 2 * g)
        z_store(DIRECT_B, g, product(4 + 2 * g))
        z_store(DIRECT_A, g, product(5 + 2 * g))
        z_start(DIRECT_B, g, right)
        z_start(DIRECT_A, g, left)

    def sums(g):
        q_wait(12 + 2 * g)
        q_wait(13 + 2 * g)
        for i in range(per_group):
            z_wait(RELAY_A, g * per_group + i)
            z_wait(RELAY_B, g * per_group + i)
        for message, arrived, slot in ((SUM_A, RELAY_A, 12 + 2 * g), (SUM_B, RELAY_B, 13 + 2 * g)):
            mine = product(slot)
            for i in range(per_group):
                k = g * per_group + i
                value = mine[:, i * width : (i + 1) * width] + z_value(arrived, k)
                zsend[message, k] = encode(value, GRAD_CODE)
        z_start(SUM_A, g, right)
        z_start(SUM_B, g, left)

    direct(0)
    for g in range(groups):
        for half in range(2):
            q_wait(8 + 2 * g + half)
        for half in range(2):
            own_ref[half, g] = product(8 + 2 * g + half)
    sums(0)
    direct(1)
    sums(1)
    m_copy.wait()

    def g_copy(head):
        owner = owner_of(head)
        slot = lax.rem(c - owner + cols - 1 + cols, cols)
        return pltpu.make_async_remote_copy(
            src_ref=gsend.at[head],
            dst_ref=grecv.at[slot],
            send_sem=gsend_sem.at[head],
            recv_sem=grecv_sem.at[slot],
            device_id={"cols": owner},
            device_id_type=MESH,
        )

    def finish(k, carry):
        g = k // per_group
        inside = pl.multiple_of(lax.rem(k, per_group) * width, width)
        for message in (DIRECT_A, SUM_A, DIRECT_B, SUM_B):
            z_wait(message, k)
        done = []
        for half, (first, second) in enumerate(((DIRECT_A, SUM_A), (DIRECT_B, SUM_B))):
            total = own_ref[half, g, :, pl.ds(inside, width)] + (z_value(first, k) + z_value(second, k))
            for j in range(per_chunk):
                head = half * half_heads + k * per_chunk + j
                start = pl.multiple_of(head * HEAD, HEAD)
                block = m_ref[pl.ds(start, HEAD), :] * MOMENTUM_DECAY + total[:, j * HEAD : (j + 1) * HEAD].T
                nm_ref[pl.ds(start, HEAD), :] = block
                high, low = split(block)
                gram = dot_nt(high, high) + (dot_nt(high, low) + dot_nt(low, high))
                diagonal = jnp.sum(gram * identity, axis=0, keepdims=True)
                gsend[head, pl.ds(0, HALF), :] = encode(pack(gram), GRAM_CODE)
                gsend[head, pl.ds(HALF, 16), :] = encode(jnp.broadcast_to(diagonal, (16, HEAD)), GRAM_CODE)
                done.append(head)
        for head in done:

            @pl.when(c != owner_of(head))
            def _():
                g_copy(head).start()

        return carry

    lax.fori_loop(0, chunks, finish, 0)

    def f_copy(step):
        return pltpu.make_async_remote_copy(
            src_ref=fsend,
            dst_ref=frecv.at[own_head],
            send_sem=fsend_sem.at[step],
            recv_sem=frecv_sem.at[own_head],
            device_id={"cols": lax.rem(c + step, cols)},
            device_id_type=MESH,
        )

    @pl.when(is_owner)
    def _():
        def arrived(slot):
            pltpu.make_async_remote_copy(
                src_ref=gsend.at[0],
                dst_ref=grecv.at[slot],
                send_sem=gsend_sem.at[0],
                recv_sem=grecv_sem.at[slot],
                device_id={"cols": lax.rem(c + 1, cols)},
                device_id_type=MESH,
            ).wait_recv()

        def add(index, total):
            for i in range(4):
                arrived(4 * index + i)
            parts = [decode(grecv[4 * index + i], GRAM_CODE) for i in range(4)]
            return total + ((parts[0] + parts[1]) + (parts[2] + parts[3]))

        sums4 = (cols - 1) // 4
        total = lax.fori_loop(0, sums4, add, decode(gsend[own_head], GRAM_CODE))
        for slot in range(4 * sums4, cols - 1):
            arrived(slot)
        for slot in range(4 * sums4, cols - 1):
            total += decode(grecv[slot], GRAM_CODE)
        diagonal = total[HALF : HALF + 1]
        gram = unpack(total[:HALF]) + identity * diagonal
        norm = jnp.sqrt(jnp.sum(diagonal, axis=1, keepdims=True)) + NORM_EPS
        current = gram / (norm * norm)
        factor = None
        for sweep in range(STEPS):
            parts = split(current)
            square = mul3(parts, parts)
            poly = C1 * identity + C3 * current + C5 * square
            poly_parts = split(poly)
            factor = poly if factor is None else mul3(poly_parts, split(factor))
            if sweep + 1 < STEPS:
                inner = mul3(parts, poly_parts)
                current = mul3(poly_parts, split(inner))
        diagonal = jnp.sum(factor * identity, axis=0, keepdims=True)
        mean = jnp.sum(diagonal, axis=1, keepdims=True) * (1.0 / HEAD)
        fsend[pl.ds(0, HALF), :] = encode(pack(factor), ROOT_CODE)
        pieces = jnp.broadcast_to(encode(diagonal - mean, ROOT_CODE).astype(F32), (16, HEAD))
        for first, rest in ((1, norm), (4, mean)):
            rest = jnp.broadcast_to(rest, (16, HEAD))
            for piece in range(3):
                part = rest.astype(BF16).astype(F32)
                pieces = jnp.where(which == first + piece, part, pieces)
                rest = rest - part
        fsend[pl.ds(HALF, 16), :] = pieces.astype(BF16)

        def send(step, carry):
            f_copy(step).start()
            return carry

        lax.fori_loop(1, cols, send, 0)
        frecv[own_head] = fsend[...]

    def apply(k, carry):
        members = [half * half_heads + k * per_chunk + j for half in range(2) for j in range(per_chunk)]
        for head in members:

            @pl.when(c != owner_of(head))
            def _():
                pltpu.make_async_remote_copy(
                    src_ref=fsend,
                    dst_ref=frecv.at[head],
                    send_sem=fsend_sem.at[0],
                    recv_sem=frecv_sem.at[head],
                    device_id={"cols": lax.rem(c + 1, cols)},
                    device_id_type=MESH,
                ).wait_recv()

        for head in members:
            pieces = frecv[head, pl.ds(HALF, 16), :].astype(F32)
            norm = pieces[1:2, :] + (pieces[2:3, :] + pieces[3:4, :])
            mean = pieces[4:5, :] + (pieces[5:6, :] + pieces[6:7, :])
            diagonal = decode(pieces[0:8, :], ROOT_CODE)[0:1] + mean
            factor = unpack(decode(frecv[head, pl.ds(0, HALF), :], ROOT_CODE)) + identity * diagonal
            start = pl.multiple_of(head * HEAD, HEAD)
            block = nm_ref[pl.ds(start, HEAD), :]
            scale = math.sqrt(cols * HEAD) / norm
            up_ref[pl.ds(start, HEAD), :] = mul3(split(factor), split(block)) * scale
        return carry

    lax.fori_loop(0, chunks, apply, 0)

    def z_drain(k, carry):
        for message in range(6):
            z_copy(message, k, right).wait_send()
        return carry

    lax.fori_loop(0, chunks, z_drain, 0)

    def g_drain(head, carry):
        @pl.when(c != owner_of(head))
        def _():
            g_copy(head).wait_send()

        return carry

    lax.fori_loop(0, heads, g_drain, 0)

    @pl.when(is_owner)
    def _():
        def f_drain(step, carry):
            f_copy(step).wait_send()
            return carry

        lax.fori_loop(1, cols, f_drain, 0)


def shards(cols, chunks, inputs, query_grads, momentum):
    rows = momentum.shape[0]
    heads = rows // HEAD
    width = rows // (2 * chunks)
    wide = rows // 4
    tokens = inputs.shape[0]
    dims = (cols, heads, chunks, width)
    out = pltpu.VMEM((rows, HEAD), F32)
    return pl.pallas_call(
        functools.partial(kernel, dims),
        out_shape=(out, out),
        in_specs=[pl.BlockSpec(memory_space=pltpu.HBM)] * 3,
        out_specs=(pl.BlockSpec(memory_space=pltpu.VMEM),) * 2,
        scratch_shapes=[
            pltpu.VMEM((tokens, HEAD), BF16),
            pltpu.VMEM((HEAD, tokens), BF16),
            pltpu.VMEM((16, tokens, wide), BF16),
            pltpu.VMEM((rows, HEAD), F32),
            pltpu.VMEM((2, 2, HEAD, wide), F32),
            pltpu.VMEM((6, chunks, HEAD, width), BF16),
            pltpu.VMEM((6, chunks, HEAD, width), BF16),
            pltpu.VMEM((heads, HALF + 16, HEAD), BF16),
            pltpu.VMEM((cols - 1, HALF + 16, HEAD), BF16),
            pltpu.VMEM((HALF + 16, HEAD), BF16),
            pltpu.VMEM((heads, HALF + 16, HEAD), BF16),
            pltpu.SemaphoreType.DMA,
            pltpu.SemaphoreType.DMA,
            pltpu.SemaphoreType.DMA((16,)),
            pltpu.SemaphoreType.DMA((6, chunks)),
            pltpu.SemaphoreType.DMA((6, chunks)),
            pltpu.SemaphoreType.DMA((heads,)),
            pltpu.SemaphoreType.DMA((cols - 1,)),
            pltpu.SemaphoreType.DMA((cols,)),
            pltpu.SemaphoreType.DMA((heads,)),
        ],
        compiler_params=pltpu.CompilerParams(
            collective_id=0, has_side_effects=True, vmem_limit_bytes=50 * 2**20
        ),
    )(*(pltpu.with_memory_space_constraint(value, pltpu.HBM) for value in (inputs, query_grads, momentum)))


def solution(mesh):
    placed = (P("dp", "cols"), P("dp", None), P("dp", "cols"))
    return jax.shard_map(
        functools.partial(shards, mesh.shape["cols"], 4),
        mesh=mesh,
        in_specs=placed,
        out_specs=(P("dp", "cols"), P("dp", "cols")),
        check_vma=False,
    )
```

time: 66.1 us -> 50.5 us (0.76)
  Pallas kernels: 60.7 us -> 47.8 us
  local copies, waits for them, and re-layouts: 4.52 us -> 1.94 us
    pallas_call x1, Pallas kernels: 60.7 us -> 47.8 us  [shards(): pl.pallas_call(functools.partial(kernel, dims), out_shape=(out, out), in_...]
    unnamed x2, local copies, waits for them, and re-layouts: 4.52 us -> 1.94 us
where the time goes in v2:
time: 50.5 us; the launch traced here: 50.4 us
  Pallas kernels  47.8 us (95%)
  local copies, waits for them, and re-layouts  1.94 us (4%)
  between operations  0.64 us (1%)
    pallas_call x1, Pallas kernels, shards(): pl.pallas_call(functools.partial(kernel, dims), out_shape=(out, out), in_...  47.8 us
    unnamed x2, local copies, waits for them, and re-layouts  1.94 us

profile of v2, /device:TPU:1, one launch (start us, length us, event | category | flops | bytes accessed | tf_op | source)
XLA Modules:
  0.0 50.4 jit_solution(16545069569330509049)
XLA Ops:
  0.6 47.8 %shard_map.50 = (f32[2048,128]{1,0:T(8,128)S(1)}, f32[2048,128]{1,0:T(8,128)S(1)}) custom-call(bf16[1024,128]{1,0:T(8,128)(2,1)} %x_hbm.1, bf16[1024,8192]{1,0:T(8,128)(2,1)} %q_hbm.1, f32[2048,128]{1,0:T(8,128)} %m_hbm.1), custom_call_target="tpu_custom_call" | custom-call | tf_op jit(solution)/shard_map/pallas_call | solution.py:419
  48.4 1.0 %copy.7 = f32[2048,128]{1,0:T(8,128)} copy(f32[2048,128]{1,0:T(8,128)S(1)} %get-tuple-element.2) | data formatting | bytes 2097152
  49.4 1.0 %copy.8 = f32[2048,128]{1,0:T(8,128)} copy(f32[2048,128]{1,0:T(8,128)S(1)} %get-tuple-element.3) | data formatting | bytes 2097152

commit v3 on v2

--- a/solution.py
+++ b/solution.py
@@ -59,7 +59,7 @@
 def mul3(a, b):
     ah, al = a
     bh, bl = b
-    return dot_nn(ah, bh) + (dot_nn(ah, bl) + dot_nn(al, bh))
+    return dot_nn(jnp.concatenate([ah, al, ah, al], axis=1), jnp.concatenate([bh, bh, bl, bl], axis=0))
 
 
 def iotas(rows):
@@ -109,12 +109,15 @@
     grecv_sem,
     fsend_sem,
     frecv_sem,
+    rows_sem,
+    plane_sem,
 ):
     cols, heads, chunks, width = dims
     half_rows = chunks * width
     rows = 2 * half_rows
     per_chunk = width // HEAD
     half_heads = heads // 2
+    side = math.isqrt(cols // 2)
     groups = 2
     wide = half_rows // groups
     per_group = chunks // groups
@@ -159,15 +162,16 @@
     m_copy = pltpu.make_async_copy(m_hbm, m_ref, m_sem)
     m_copy.start()
 
+    core = lax.rem(c, 2)
+    along_y = lax.rem(c // 2, side)
+    along_x = c // (2 * side)
+    other_core = c + 1 - 2 * core
+    row_peers = [(lax.rem(along_x + i, side) * side + along_y) * 2 + core for i in range(1, side)]
+    column_peers = [(along_x * side + lax.rem(along_y + i, side)) * 2 + core for i in range(1, side)]
     barrier = pltpu.get_barrier_semaphore()
-    for step in (1, 3):
-        pl.semaphore_signal(barrier, inc=1, device_id={"dp": lax.rem(z + step, 4)}, device_id_type=MESH)
-
-    def greet(step, carry):
-        pl.semaphore_signal(barrier, inc=1, device_id={"cols": lax.rem(c + step, cols)}, device_id_type=MESH)
-        return carry
-
-    lax.fori_loop(1, cols, greet, 0)
+    near = [{"dp": right}, {"dp": left}] + [{"cols": peer} for peer in row_peers + column_peers + [other_core]]
+    for peer in near:
+        pl.semaphore_signal(barrier, inc=1, device_id=peer, device_id_type=MESH)
 
     x_copy.wait()
     xt_ref[...] = x_ref[...].T
@@ -204,12 +208,12 @@
 
     for g in range(groups):
         q_wait(2 * g)
+        z_store(RELAY_A, g, product(2 * g))
+        if g == 0:
+            pl.semaphore_wait(barrier, len(near))
+        z_start(RELAY_A, g, right)
         q_wait(2 * g + 1)
-        z_store(RELAY_A, g, product(2 * g))
         z_store(RELAY_B, g, product(2 * g + 1))
-        if g == 0:
-            pl.semaphore_wait(barrier, cols - 1 + 2)
-        z_start(RELAY_A, g, right)
         z_start(RELAY_B, g, left)
 
     def direct(g):
@@ -235,7 +239,11 @@
         z_start(SUM_A, g, right)
         z_start(SUM_B, g, left)
 
+    for peer in column_peers:
+        pl.semaphore_signal(rows_sem, inc=1, device_id={"cols": peer}, device_id_type=MESH)
     direct(0)
+    pl.semaphore_wait(rows_sem, side - 1)
+    pl.semaphore_signal(plane_sem, inc=1, device_id={"cols": other_core}, device_id_type=MESH)
     for g in range(groups):
         for half in range(2):
             q_wait(8 + 2 * g + half)
@@ -245,6 +253,7 @@
     direct(1)
     sums(1)
     m_copy.wait()
+    pl.semaphore_wait(plane_sem, 1)
 
     def g_copy(head):
         owner = owner_of(head)
@@ -272,7 +281,9 @@
                 block = m_ref[pl.ds(start, HEAD), :] * MOMENTUM_DECAY + total[:, j * HEAD : (j + 1) * HEAD].T
                 nm_ref[pl.ds(start, HEAD), :] = block
                 high, low = split(block)
-                gram = dot_nt(high, high) + (dot_nt(high, low) + dot_nt(low, high))
+                gram = dot_nt(
+                    jnp.concatenate([high, low, high, low], axis=1), jnp.concatenate([high, high, low, low], axis=1)
+                )
                 diagonal = jnp.sum(gram * identity, axis=0, keepdims=True)
                 gsend[head, pl.ds(0, HALF), :] = encode(pack(gram), GRAM_CODE)
                 gsend[head, pl.ds(HALF, 16), :] = encode(jnp.broadcast_to(diagonal, (16, HEAD)), GRAM_CODE)
@@ -408,6 +419,14 @@
         lax.fori_loop(1, cols, f_drain, 0)
 
 
+def write_out(nm_ref, up_ref, nm_hbm, up_hbm, nm_sem, up_sem):
+    copies = [pltpu.make_async_copy(nm_ref, nm_hbm, nm_sem), pltpu.make_async_copy(up_ref, up_hbm, up_sem)]
+    for copy in copies:
+        copy.start()
+    for copy in copies:
+        copy.wait()
+
+
 def shards(cols, chunks, inputs, query_grads, momentum):
     rows = momentum.shape[0]
     heads = rows // HEAD
@@ -416,7 +435,7 @@
     tokens = inputs.shape[0]
     dims = (cols, heads, chunks, width)
     out = pltpu.VMEM((rows, HEAD), F32)
-    return pl.pallas_call(
+    done = pl.pallas_call(
         functools.partial(kernel, dims),
         out_shape=(out, out),
         in_specs=[pl.BlockSpec(memory_space=pltpu.HBM)] * 3,
@@ -442,11 +461,21 @@
             pltpu.SemaphoreType.DMA((cols - 1,)),
             pltpu.SemaphoreType.DMA((cols,)),
             pltpu.SemaphoreType.DMA((heads,)),
+            pltpu.SemaphoreType.REGULAR,
+            pltpu.SemaphoreType.REGULAR,
         ],
         compiler_params=pltpu.CompilerParams(
             collective_id=0, has_side_effects=True, vmem_limit_bytes=50 * 2**20
         ),
     )(*(pltpu.with_memory_space_constraint(value, pltpu.HBM) for value in (inputs, query_grads, momentum)))
+    return pl.pallas_call(
+        write_out,
+        out_shape=(jax.ShapeDtypeStruct((rows, HEAD), F32),) * 2,
+        in_specs=[pl.BlockSpec(memory_space=pltpu.VMEM)] * 2,
+        out_specs=(pl.BlockSpec(memory_space=pltpu.HBM),) * 2,
+        scratch_shapes=[pltpu.SemaphoreType.DMA, pltpu.SemaphoreType.DMA],
+        compiler_params=pltpu.CompilerParams(vmem_limit_bytes=2**20),
+    )(*done)
 
 
 def solution(mesh):

time: 50.5 us -> 49.6 us (0.982)
  local copies, waits for them, and re-layouts: 1.94 us -> 0 us
  Pallas kernels: 47.8 us -> 48.9 us
    unnamed x2 -> x0, local copies, waits for them, and re-layouts: 1.94 us -> none
    pallas_call x0 -> x1, Pallas kernels: none -> 1.33 us  [shards(): pl.pallas_call(write_out, out_shape=(jax.ShapeDtypeStruct((rows, HEAD), F...]
where the time goes in v3:
time: 49.6 us; the launch traced here: 49.5 us
  Pallas kernels  48.9 us (99%)
  between operations  0.64 us (1%)
    pallas_call x1, Pallas kernels, shards(): pl.pallas_call(functools.partial(kernel, dims), out_shape=(out, out), in_...  47.6 us
    pallas_call x1, Pallas kernels, shards(): pl.pallas_call(write_out, out_shape=(jax.ShapeDtypeStruct((rows, HEAD), F...  1.33 us

profile of v3, /device:TPU:1, one launch (start us, length us, event | category | flops | bytes accessed | tf_op | source)
XLA Modules:
  0.0 49.5 jit_solution(6987907126305569944)
XLA Ops:
  0.6 47.6 %shard_map.50 = (f32[2048,128]{1,0:T(8,128)S(1)}, f32[2048,128]{1,0:T(8,128)S(1)}) custom-call(bf16[1024,128]{1,0:T(8,128)(2,1)} %x_hbm.1, bf16[1024,8192]{1,0:T(8,128)(2,1)} %q_hbm.1, f32[2048,128]{1,0:T(8,128)} %m_hbm.1), custom_call_target="tpu_custom_call" | custom-call | tf_op jit(solution)/shard_map/pallas_call | solution.py:438
  48.2 1.3 %shard_map.51 = (f32[2048,128]{1,0:T(8,128)}, f32[2048,128]{1,0:T(8,128)}) custom-call(f32[2048,128]{1,0:T(8,128)S(1)} %get-tuple-element.4.nm_ref, f32[2048,128]{1,0:T(8,128)S(1)} %get-tuple-element.5.up_ref), custom_call_target="tpu_custom_call" | custom-call | tf_op jit(solution)/shard_map/pallas_call | solution.py:471

commit v4 on v3

--- a/solution.py
+++ b/solution.py
@@ -11,6 +11,7 @@
 HEAD = 128
 HALF = HEAD // 2
 STEPS = 5
+AHEAD = 3
 MOMENTUM_DECAY = 0.95
 NORM_EPS = 1e-07
 C1 = 3.4445
@@ -109,8 +110,7 @@
     grecv_sem,
     fsend_sem,
     frecv_sem,
-    rows_sem,
-    plane_sem,
+    round_sem,
 ):
     cols, heads, chunks, width = dims
     half_rows = chunks * width
@@ -145,39 +145,49 @@
         start = pl.multiple_of(target * rows + half * half_rows + g * wide, wide)
         return pltpu.make_async_copy(q_hbm.at[:, pl.ds(start, wide)], q_ref.at[slot], q_sem.at[slot])
 
-    for g in range(groups):
-        q_copy(2 * g, opposite, 0, g).start()
-        q_copy(2 * g + 1, opposite, 1, g).start()
-    q_copy(4, right, 1, 0).start()
-    q_copy(5, left, 0, 0).start()
-    for g in range(groups):
-        q_copy(8 + 2 * g, z, 0, g).start()
-        q_copy(9 + 2 * g, z, 1, g).start()
-    q_copy(12, right, 0, 0).start()
-    q_copy(13, left, 1, 0).start()
-    q_copy(6, right, 1, 1).start()
-    q_copy(7, left, 0, 1).start()
-    q_copy(14, right, 0, 1).start()
-    q_copy(15, left, 1, 1).start()
+    blocks = [(opposite, 0, 0), (opposite, 1, 0), (opposite, 0, 1), (opposite, 1, 1)]
+    blocks += [(right, 1, 0), (left, 0, 0), (z, 0, 0), (z, 1, 0), (z, 0, 1), (z, 1, 1)]
+    blocks += [(right, 0, 0), (left, 1, 0), (right, 1, 1), (left, 0, 1), (right, 0, 1), (left, 1, 1)]
+    direct_slots = (4, 12)
+    own_slots = (6, 8)
+    sum_slots = (10, 14)
+    for slot in range(AHEAD):
+        q_copy(slot, *blocks[slot]).start()
     m_copy = pltpu.make_async_copy(m_hbm, m_ref, m_sem)
-    m_copy.start()
 
     core = lax.rem(c, 2)
     along_y = lax.rem(c // 2, side)
     along_x = c // (2 * side)
-    other_core = c + 1 - 2 * core
-    row_peers = [(lax.rem(along_x + i, side) * side + along_y) * 2 + core for i in range(1, side)]
-    column_peers = [(along_x * side + lax.rem(along_y + i, side)) * 2 + core for i in range(1, side)]
+
+    def device(dx, dy, dc):
+        return (lax.rem(along_x + dx, side) * side + lax.rem(along_y + dy, side)) * 2 + lax.rem(core + dc, 2)
+
+    row_peers = [device(1, 0, 0), device(side - 1, 0, 0)]
+    column_peers = [device(0, 1, 0), device(0, side - 1, 0)]
+    other_core = device(0, 0, 1)
     barrier = pltpu.get_barrier_semaphore()
     near = [{"dp": right}, {"dp": left}] + [{"cols": peer} for peer in row_peers + column_peers + [other_core]]
     for peer in near:
         pl.semaphore_signal(barrier, inc=1, device_id=peer, device_id_type=MESH)
 
+    rounds = (row_peers, column_peers, column_peers, [other_core])
+
+    def tell(index):
+        for peer in rounds[index]:
+            pl.semaphore_signal(round_sem.at[index], inc=1, device_id={"cols": peer}, device_id_type=MESH)
+
+    def heard(index):
+        pl.semaphore_wait(round_sem.at[index], len(rounds[index]))
+
     x_copy.wait()
     xt_ref[...] = x_ref[...].T
 
     def q_wait(slot):
-        pltpu.make_async_copy(q_hbm.at[:, pl.ds(0, wide)], q_ref.at[slot], q_sem.at[slot]).wait()
+        q_copy(slot, *blocks[slot]).wait()
+        if slot + AHEAD < len(blocks):
+            q_copy(slot + AHEAD, *blocks[slot + AHEAD]).start()
+        elif slot + 1 == len(blocks):
+            m_copy.start()
 
     def product(slot):
         return dot_nn(xt_ref[...], q_ref[slot])
@@ -206,31 +216,41 @@
     def z_value(message, k):
         return decode(zrecv[message, k], GRAD_CODE)
 
-    for g in range(groups):
+    for half in range(2):
+        q_wait(half)
+        message, target = ((RELAY_A, right), (RELAY_B, left))[half]
+        for i in range(per_group):
+            value = dot_nn(xt_ref[...], q_ref[half, :, i * width : (i + 1) * width])
+            zsend[message, i] = encode(value, GRAD_CODE)
+            if half + i == 0:
+                pl.semaphore_wait(barrier, len(near))
+            z_copy(message, i, target).start()
+    tell(0)
+    for g in range(1, groups):
         q_wait(2 * g)
         z_store(RELAY_A, g, product(2 * g))
-        if g == 0:
-            pl.semaphore_wait(barrier, len(near))
         z_start(RELAY_A, g, right)
         q_wait(2 * g + 1)
         z_store(RELAY_B, g, product(2 * g + 1))
         z_start(RELAY_B, g, left)
 
     def direct(g):
-        q_wait(4 + 2 * g)
-        q_wait(5 + 2 * g)
-        z_store(DIRECT_B, g, product(4 + 2 * g))
-        z_store(DIRECT_A, g, product(5 + 2 * g))
+        slot = direct_slots[g]
+        q_wait(slot)
+        q_wait(slot + 1)
+        z_store(DIRECT_B, g, product(slot))
+        z_store(DIRECT_A, g, product(slot + 1))
         z_start(DIRECT_B, g, right)
         z_start(DIRECT_A, g, left)
 
     def sums(g):
-        q_wait(12 + 2 * g)
-        q_wait(13 + 2 * g)
+        first = sum_slots[g]
+        q_wait(first)
+        q_wait(first + 1)
         for i in range(per_group):
             z_wait(RELAY_A, g * per_group + i)
             z_wait(RELAY_B, g * per_group + i)
-        for message, arrived, slot in ((SUM_A, RELAY_A, 12 + 2 * g), (SUM_B, RELAY_B, 13 + 2 * g)):
+        for message, arrived, slot in ((SUM_A, RELAY_A, first), (SUM_B, RELAY_B, first + 1)):
             mine = product(slot)
             for i in range(per_group):
                 k = g * per_group + i
@@ -239,25 +259,30 @@
         z_start(SUM_A, g, right)
         z_start(SUM_B, g, left)
 
-    for peer in column_peers:
-        pl.semaphore_signal(rows_sem, inc=1, device_id={"cols": peer}, device_id_type=MESH)
+    heard(0)
+    tell(1)
     direct(0)
-    pl.semaphore_wait(rows_sem, side - 1)
-    pl.semaphore_signal(plane_sem, inc=1, device_id={"cols": other_core}, device_id_type=MESH)
+    heard(1)
+    tell(2)
     for g in range(groups):
         for half in range(2):
-            q_wait(8 + 2 * g + half)
+            q_wait(own_slots[g] + half)
         for half in range(2):
-            own_ref[half, g] = product(8 + 2 * g + half)
+            own_ref[half, g] = product(own_slots[g] + half)
+    heard(2)
+    tell(3)
     sums(0)
     direct(1)
     sums(1)
     m_copy.wait()
-    pl.semaphore_wait(plane_sem, 1)
+    heard(3)
 
     def g_copy(head):
         owner = owner_of(head)
-        slot = lax.rem(c - owner + cols - 1 + cols, cols)
+        dx = lax.rem(along_x - owner // (2 * side) + side, side)
+        dy = lax.rem(along_y - lax.rem(owner // 2, side) + side, side)
+        dc = lax.rem(core + owner, 2)
+        slot = jnp.maximum((dx * side + dy) * 2 + dc - 1, 0)
         return pltpu.make_async_remote_copy(
             src_ref=gsend.at[head],
             dst_ref=grecv.at[slot],
@@ -298,13 +323,18 @@
 
     lax.fori_loop(0, chunks, finish, 0)
 
+    others = sorted(
+        ((dx, dy, dc) for dx in range(side) for dy in range(side) for dc in range(2) if dx + dy + dc),
+        key=lambda d: (min(d[0], side - d[0]) + min(d[1], side - d[1]), d[2]),
+    )
+
     def f_copy(step):
         return pltpu.make_async_remote_copy(
             src_ref=fsend,
             dst_ref=frecv.at[own_head],
             send_sem=fsend_sem.at[step],
             recv_sem=frecv_sem.at[own_head],
-            device_id={"cols": lax.rem(c + step, cols)},
+            device_id={"cols": device(*others[step])},
             device_id_type=MESH,
         )
 
@@ -320,18 +350,13 @@
                 device_id_type=MESH,
             ).wait_recv()
 
-        def add(index, total):
-            for i in range(4):
-                arrived(4 * index + i)
-            parts = [decode(grecv[4 * index + i], GRAM_CODE) for i in range(4)]
-            return total + ((parts[0] + parts[1]) + (parts[2] + parts[3]))
-
-        sums4 = (cols - 1) // 4
-        total = lax.fori_loop(0, sums4, add, decode(gsend[own_head], GRAM_CODE))
-        for slot in range(4 * sums4, cols - 1):
-            arrived(slot)
-        for slot in range(4 * sums4, cols - 1):
-            total += decode(grecv[slot], GRAM_CODE)
+        slots = [(dx * side + dy) * 2 + dc - 1 for dx, dy, dc in others]
+        total = decode(gsend[own_head], GRAM_CODE)
+        for first in range(0, cols - 1, 4):
+            for slot in slots[first : first + 4]:
+                arrived(slot)
+            for slot in slots[first : first + 4]:
+                total += decode(grecv[slot], GRAM_CODE)
         diagonal = total[HALF : HALF + 1]
         gram = unpack(total[:HALF]) + identity * diagonal
         norm = jnp.sqrt(jnp.sum(diagonal, axis=1, keepdims=True)) + NORM_EPS
@@ -358,11 +383,8 @@
                 rest = rest - part
         fsend[pl.ds(HALF, 16), :] = pieces.astype(BF16)
 
-        def send(step, carry):
+        for step in reversed(range(cols - 1)):
             f_copy(step).start()
-            return carry
-
-        lax.fori_loop(1, cols, send, 0)
         frecv[own_head] = fsend[...]
 
     def apply(k, carry):
@@ -392,8 +414,6 @@
             up_ref[pl.ds(start, HEAD), :] = mul3(split(factor), split(block)) * scale
         return carry
 
-    lax.fori_loop(0, chunks, apply, 0)
-
     def z_drain(k, carry):
         for message in range(6):
             z_copy(message, k, right).wait_send()
@@ -409,14 +429,14 @@
         return carry
 
     lax.fori_loop(0, heads, g_drain, 0)
+    lax.fori_loop(0, chunks - 1, apply, 0)
 
     @pl.when(is_owner)
     def _():
-        def f_drain(step, carry):
+        for step in range(cols - 1):
             f_copy(step).wait_send()
-            return carry
-
-        lax.fori_loop(1, cols, f_drain, 0)
+
+    apply(chunks - 1, 0)
 
 
 def write_out(nm_ref, up_ref, nm_hbm, up_hbm, nm_sem, up_sem):
@@ -461,8 +481,7 @@
             pltpu.SemaphoreType.DMA((cols - 1,)),
             pltpu.SemaphoreType.DMA((cols,)),
             pltpu.SemaphoreType.DMA((heads,)),
-            pltpu.SemaphoreType.REGULAR,
-            pltpu.SemaphoreType.REGULAR,
+            pltpu.SemaphoreType.REGULAR((4,)),
         ],
         compiler_params=pltpu.CompilerParams(
             collective_id=0, has_side_effects=True, vmem_limit_bytes=50 * 2**20

time: 49.6 us -> 44.8 us (0.903)
  Pallas kernels: 48.9 us -> 44 us
    pallas_call x1, Pallas kernels: 47.6 us -> 42.7 us  [shards(): pl.pallas_call(functools.partial(kernel, dims), out_shape=(out, out), in_...]
where the time goes in v4:
time: 44.8 us; the launch traced here: 44.7 us
  Pallas kernels  44 us (98%)
  between operations  0.64 us (1%)
    pallas_call x1, Pallas kernels, shards(): pl.pallas_call(functools.partial(kernel, dims), out_shape=(out, out), in_...  42.7 us
    pallas_call x1, Pallas kernels, shards(): pl.pallas_call(write_out, out_shape=(jax.ShapeDtypeStruct((rows, HEAD), F...  1.33 us

profile of v4, /device:TPU:1, one launch (start us, length us, event | category | flops | bytes accessed | tf_op | source)
XLA Modules:
  0.0 44.7 jit_solution(8438825813016832744)
XLA Ops:
  0.6 42.7 %shard_map.50 = (f32[2048,128]{1,0:T(8,128)S(1)}, f32[2048,128]{1,0:T(8,128)S(1)}) custom-call(bf16[1024,128]{1,0:T(8,128)(2,1)} %x_hbm.1, bf16[1024,8192]{1,0:T(8,128)(2,1)} %q_hbm.1, f32[2048,128]{1,0:T(8,128)} %m_hbm.1), custom_call_target="tpu_custom_call" | custom-call | tf_op jit(solution)/shard_map/pallas_call | solution.py:458
  43.3 1.3 %shard_map.51 = (f32[2048,128]{1,0:T(8,128)}, f32[2048,128]{1,0:T(8,128)}) custom-call(f32[2048,128]{1,0:T(8,128)S(1)} %get-tuple-element.4.nm_ref, f32[2048,128]{1,0:T(8,128)S(1)} %get-tuple-element.5.up_ref), custom_call_target="tpu_custom_call" | custom-call | tf_op jit(solution)/shard_map/pallas_call | solution.py:490

commit v5 on v4

--- a/solution.py
+++ b/solution.py
@@ -23,6 +23,7 @@
 
 GRAD_CODE = (0.125, 2.0**-6, 4)
 GRAM_CODE = (8.0, 2.0**-12, 3)
+ROW_CODE = (64.0, 2.0**-12, 3)
 ROOT_CODE = (0.0625, 2.0**-6, 4)
 RELAY_A, RELAY_B, DIRECT_B, DIRECT_A, SUM_A, SUM_B = range(6)
 
@@ -99,6 +100,8 @@
     zrecv,
     gsend,
     grecv,
+    rsend,
+    rrecv,
     fsend,
     frecv,
     x_sem,
@@ -108,6 +111,8 @@
     zrecv_sem,
     gsend_sem,
     grecv_sem,
+    rsend_sem,
+    rrecv_sem,
     fsend_sem,
     frecv_sem,
     round_sem,
@@ -128,15 +133,9 @@
     left = lax.rem(z + 3, 4)
     opposite = lax.rem(z + 2, 4)
 
-    own_head = c // 2
-    is_owner = jnp.logical_and(own_head < heads, lax.rem(c, 2) == lax.rem(own_head, 2))
-
     row, lane = iotas(HEAD)
     identity = jnp.where(row == lane, 1.0, 0.0)
     which = iotas(16)[0]
-
-    def owner_of(head):
-        return 2 * head + lax.rem(head, 2)
 
     x_copy = pltpu.make_async_copy(x_hbm, x_ref, x_sem)
     x_copy.start()
@@ -170,7 +169,7 @@
     for peer in near:
         pl.semaphore_signal(barrier, inc=1, device_id=peer, device_id_type=MESH)
 
-    rounds = (row_peers, column_peers, column_peers, [other_core])
+    rounds = (row_peers + column_peers, [other_core])
 
     def tell(index):
         for peer in rounds[index]:
@@ -262,33 +261,39 @@
     heard(0)
     tell(1)
     direct(0)
-    heard(1)
-    tell(2)
     for g in range(groups):
         for half in range(2):
             q_wait(own_slots[g] + half)
         for half in range(2):
             own_ref[half, g] = product(own_slots[g] + half)
-    heard(2)
-    tell(3)
     sums(0)
     direct(1)
     sums(1)
     m_copy.wait()
-    heard(3)
-
-    def g_copy(head):
-        owner = owner_of(head)
-        dx = lax.rem(along_x - owner // (2 * side) + side, side)
-        dy = lax.rem(along_y - lax.rem(owner // 2, side) + side, side)
-        dc = lax.rem(core + owner, 2)
-        slot = jnp.maximum((dx * side + dy) * 2 + dc - 1, 0)
+    heard(1)
+
+    members = 2 * per_chunk
+
+    def head_of(k, m):
+        return (m // per_chunk) * half_heads + k * per_chunk + m % per_chunk
+
+    def owned_head(turn):
+        k = core + 2 * turn
+        return (along_x // per_chunk) * half_heads + k * per_chunk + lax.rem(along_x, per_chunk)
+
+    def is_mine(k, m):
+        return jnp.logical_and(along_x == m, core == lax.rem(k, 2))
+
+    def g_copy(k, m):
+        head = head_of(k, m)
+        dx = lax.rem(along_x - m + side, side)
+        slot = jnp.maximum(dx * 2 + lax.rem(core + k, 2) - 1, 0)
         return pltpu.make_async_remote_copy(
             src_ref=gsend.at[head],
-            dst_ref=grecv.at[slot],
+            dst_ref=grecv.at[k // 2, slot],
             send_sem=gsend_sem.at[head],
-            recv_sem=grecv_sem.at[slot],
-            device_id={"cols": owner},
+            recv_sem=grecv_sem.at[k // 2, slot],
+            device_id={"cols": (m * side + along_y) * 2 + lax.rem(k, 2)},
             device_id_type=MESH,
         )
 
@@ -297,7 +302,6 @@
         inside = pl.multiple_of(lax.rem(k, per_group) * width, width)
         for message in (DIRECT_A, SUM_A, DIRECT_B, SUM_B):
             z_wait(message, k)
-        done = []
         for half, (first, second) in enumerate(((DIRECT_A, SUM_A), (DIRECT_B, SUM_B))):
             total = own_ref[half, g, :, pl.ds(inside, width)] + (z_value(first, k) + z_value(second, k))
             for j in range(per_chunk):
@@ -312,51 +316,62 @@
                 diagonal = jnp.sum(gram * identity, axis=0, keepdims=True)
                 gsend[head, pl.ds(0, HALF), :] = encode(pack(gram), GRAM_CODE)
                 gsend[head, pl.ds(HALF, 16), :] = encode(jnp.broadcast_to(diagonal, (16, HEAD)), GRAM_CODE)
-                done.append(head)
-        for head in done:
-
-            @pl.when(c != owner_of(head))
+        for m in range(members):
+
+            @pl.when(jnp.logical_not(is_mine(k, m)))
             def _():
-                g_copy(head).start()
+                g_copy(k, m).start()
 
         return carry
 
-    lax.fori_loop(0, chunks, finish, 0)
-
-    others = sorted(
-        ((dx, dy, dc) for dx in range(side) for dy in range(side) for dc in range(2) if dx + dy + dc),
-        key=lambda d: (min(d[0], side - d[0]) + min(d[1], side - d[1]), d[2]),
-    )
-
-    def f_copy(step):
+    along_row = sorted(((dx, dc) for dx in range(side) for dc in range(2) if dx + dc), key=lambda d: min(d[0], side - d[0]))
+    along_column = range(1, side)
+
+    def r_copy(turn, dy):
         return pltpu.make_async_remote_copy(
-            src_ref=fsend,
-            dst_ref=frecv.at[own_head],
-            send_sem=fsend_sem.at[step],
-            recv_sem=frecv_sem.at[own_head],
-            device_id={"cols": device(*others[step])},
+            src_ref=rsend.at[turn],
+            dst_ref=rrecv.at[turn, dy - 1],
+            send_sem=rsend_sem.at[turn, dy - 1],
+            recv_sem=rrecv_sem.at[turn, dy - 1],
+            device_id={"cols": device(0, dy, 0)},
             device_id_type=MESH,
         )
 
-    @pl.when(is_owner)
-    def _():
-        def arrived(slot):
+    def row_sum(turn):
+        total = decode(gsend[owned_head(turn)], GRAM_CODE)
+        for dx, dc in along_row:
+            slot = dx * 2 + dc - 1
             pltpu.make_async_remote_copy(
                 src_ref=gsend.at[0],
-                dst_ref=grecv.at[slot],
+                dst_ref=grecv.at[turn, slot],
                 send_sem=gsend_sem.at[0],
-                recv_sem=grecv_sem.at[slot],
-                device_id={"cols": lax.rem(c + 1, cols)},
+                recv_sem=grecv_sem.at[turn, slot],
+                device_id={"cols": other_core},
                 device_id_type=MESH,
             ).wait_recv()
-
-        slots = [(dx * side + dy) * 2 + dc - 1 for dx, dy, dc in others]
-        total = decode(gsend[own_head], GRAM_CODE)
-        for first in range(0, cols - 1, 4):
-            for slot in slots[first : first + 4]:
-                arrived(slot)
-            for slot in slots[first : first + 4]:
-                total += decode(grecv[slot], GRAM_CODE)
+            total += decode(grecv[turn, slot], GRAM_CODE)
+        rsend[turn] = encode(total, ROW_CODE)
+        for dy in (2, 1, 3):
+            r_copy(turn, dy).start()
+
+    def f_copy(turn, index):
+        head = owned_head(turn)
+        dx, dc = along_row[index]
+        return pltpu.make_async_remote_copy(
+            src_ref=fsend.at[turn],
+            dst_ref=frecv.at[head],
+            send_sem=fsend_sem.at[turn, index],
+            recv_sem=frecv_sem.at[head],
+            device_id={"cols": device(dx, 0, dc)},
+            device_id_type=MESH,
+        )
+
+    def polynomial(turn):
+        total = decode(rsend[turn], ROW_CODE)
+        for dy in along_column:
+            r_copy(turn, dy).wait_recv()
+        for dy in along_column:
+            total += decode(rrecv[turn, dy - 1], ROW_CODE)
         diagonal = total[HALF : HALF + 1]
         gram = unpack(total[:HALF]) + identity * diagonal
         norm = jnp.sqrt(jnp.sum(diagonal, axis=1, keepdims=True)) + NORM_EPS
@@ -373,7 +388,7 @@
                 current = mul3(poly_parts, split(inner))
         diagonal = jnp.sum(factor * identity, axis=0, keepdims=True)
         mean = jnp.sum(diagonal, axis=1, keepdims=True) * (1.0 / HEAD)
-        fsend[pl.ds(0, HALF), :] = encode(pack(factor), ROOT_CODE)
+        fsend[turn, pl.ds(0, HALF), :] = encode(pack(factor), ROOT_CODE)
         pieces = jnp.broadcast_to(encode(diagonal - mean, ROOT_CODE).astype(F32), (16, HEAD))
         for first, rest in ((1, norm), (4, mean)):
             rest = jnp.broadcast_to(rest, (16, HEAD))
@@ -381,28 +396,28 @@
                 part = rest.astype(BF16).astype(F32)
                 pieces = jnp.where(which == first + piece, part, pieces)
                 rest = rest - part
-        fsend[pl.ds(HALF, 16), :] = pieces.astype(BF16)
-
-        for step in reversed(range(cols - 1)):
-            f_copy(step).start()
-        frecv[own_head] = fsend[...]
+        fsend[turn, pl.ds(HALF, 16), :] = pieces.astype(BF16)
+        for index in reversed(range(len(along_row))):
+            f_copy(turn, index).start()
+        frecv[owned_head(turn)] = fsend[turn]
 
     def apply(k, carry):
-        members = [half * half_heads + k * per_chunk + j for half in range(2) for j in range(per_chunk)]
-        for head in members:
-
-            @pl.when(c != owner_of(head))
+        for m in range(members):
+
+            @pl.when(jnp.logical_not(is_mine(k, m)))
             def _():
+                head = head_of(k, m)
                 pltpu.make_async_remote_copy(
-                    src_ref=fsend,
+                    src_ref=fsend.at[0],
                     dst_ref=frecv.at[head],
-                    send_sem=fsend_sem.at[0],
+                    send_sem=fsend_sem.at[0, 0],
                     recv_sem=frecv_sem.at[head],
-                    device_id={"cols": lax.rem(c + 1, cols)},
+                    device_id={"cols": other_core},
                     device_id_type=MESH,
                 ).wait_recv()
 
-        for head in members:
+        for m in range(members):
+            head = head_of(k, m)
             pieces = frecv[head, pl.ds(HALF, 16), :].astype(F32)
             norm = pieces[1:2, :] + (pieces[2:3, :] + pieces[3:4, :])
             mean = pieces[4:5, :] + (pieces[5:6, :] + pieces[6:7, :])
@@ -419,23 +434,29 @@
             z_copy(message, k, right).wait_send()
         return carry
 
+    def g_drain(k, carry):
+        for m in range(members):
+
+            @pl.when(jnp.logical_not(is_mine(k, m)))
+            def _():
+                g_copy(k, m).wait_send()
+
+        return carry
+
+    lax.fori_loop(0, chunks - 1, finish, 0)
+    row_sum(0)
+    finish(chunks - 1, 0)
+    polynomial(0)
+    row_sum(1)
     lax.fori_loop(0, chunks, z_drain, 0)
-
-    def g_drain(head, carry):
-        @pl.when(c != owner_of(head))
-        def _():
-            g_copy(head).wait_send()
-
-        return carry
-
-    lax.fori_loop(0, heads, g_drain, 0)
+    lax.fori_loop(0, chunks, g_drain, 0)
+    polynomial(1)
     lax.fori_loop(0, chunks - 1, apply, 0)
-
-    @pl.when(is_owner)
-    def _():
-        for step in range(cols - 1):
-            f_copy(step).wait_send()
-
+    for turn in range(2):
+        for dy in along_column:
+            r_copy(turn, dy).wait_send()
+        for index in range(len(along_row)):
+            f_copy(turn, index).wait_send()
     apply(chunks - 1, 0)
 
 
@@ -454,6 +475,7 @@
     wide = rows // 4
     tokens = inputs.shape[0]
     dims = (cols, heads, chunks, width)
+    side = math.isqrt(cols // 2)
     out = pltpu.VMEM((rows, HEAD), F32)
     done = pl.pallas_call(
         functools.partial(kernel, dims),
@@ -469,8 +491,10 @@
             pltpu.VMEM((6, chunks, HEAD, width), BF16),
             pltpu.VMEM((6, chunks, HEAD, width), BF16),
             pltpu.VMEM((heads, HALF + 16, HEAD), BF16),
-            pltpu.VMEM((cols - 1, HALF + 16, HEAD), BF16),
-            pltpu.VMEM((HALF + 16, HEAD), BF16),
+            pltpu.VMEM((2, 2 * side - 1, HALF + 16, HEAD), BF16),
+            pltpu.VMEM((2, HALF + 16, HEAD), BF16),
+            pltpu.VMEM((2, side - 1, HALF + 16, HEAD), BF16),
+            pltpu.VMEM((2, HALF + 16, HEAD), BF16),
             pltpu.VMEM((heads, HALF + 16, HEAD), BF16),
             pltpu.SemaphoreType.DMA,
             pltpu.SemaphoreType.DMA,
@@ -478,10 +502,12 @@
             pltpu.SemaphoreType.DMA((6, chunks)),
             pltpu.SemaphoreType.DMA((6, chunks)),
             pltpu.SemaphoreType.DMA((heads,)),
-            pltpu.SemaphoreType.DMA((cols - 1,)),
-            pltpu.SemaphoreType.DMA((cols,)),
+            pltpu.SemaphoreType.DMA((2, 2 * side - 1)),
+            pltpu.SemaphoreType.DMA((2, side - 1)),
+            pltpu.SemaphoreType.DMA((2, side - 1)),
+            pltpu.SemaphoreType.DMA((2, 2 * side - 1)),
             pltpu.SemaphoreType.DMA((heads,)),
-            pltpu.SemaphoreType.REGULAR((4,)),
+            pltpu.SemaphoreType.REGULAR((2,)),
         ],
         compiler_params=pltpu.CompilerParams(
             collective_id=0, has_side_effects=True, vmem_limit_bytes=50 * 2**20

time: 44.8 us -> 47.6 us (1.062)
  Pallas kernels: 44 us -> 46.8 us
    pallas_call x1, Pallas kernels: 42.7 us -> 45.4 us  [shards(): pl.pallas_call(functools.partial(kernel, dims), out_shape=(out, out), in_...]
where the time goes in v5:
time: 47.6 us; the launch traced here: 47.4 us
  Pallas kernels  46.8 us (98%)
  between operations  0.64 us (1%)
    pallas_call x1, Pallas kernels, shards(): pl.pallas_call(functools.partial(kernel, dims), out_shape=(out, out), in_...  45.4 us
    pallas_call x1, Pallas kernels, shards(): pl.pallas_call(write_out, out_shape=(jax.ShapeDtypeStruct((rows, HEAD), F...  1.33 us

profile of v5, /device:TPU:1, one launch (start us, length us, event | category | flops | bytes accessed | tf_op | source)
XLA Modules:
  0.0 47.4 jit_solution(16668553511421032489)
XLA Ops:
  0.6 45.4 %shard_map.50 = (f32[2048,128]{1,0:T(8,128)S(1)}, f32[2048,128]{1,0:T(8,128)S(1)}) custom-call(bf16[1024,128]{1,0:T(8,128)(2,1)} %x_hbm.1, bf16[1024,8192]{1,0:T(8,128)(2,1)} %q_hbm.1, f32[2048,128]{1,0:T(8,128)} %m_hbm.1), custom_call_target="tpu_custom_call" | custom-call | tf_op jit(solution)/shard_map/pallas_call | solution.py:480
  46.1 1.3 %shard_map.51 = (f32[2048,128]{1,0:T(8,128)}, f32[2048,128]{1,0:T(8,128)}) custom-call(f32[2048,128]{1,0:T(8,128)S(1)} %get-tuple-element.4.nm_ref, f32[2048,128]{1,0:T(8,128)S(1)} %get-tuple-element.5.up_ref), custom_call_target="tpu_custom_call" | custom-call | tf_op jit(solution)/shard_map/pallas_call | solution.py:516

commit v6 on v4

--- a/solution.py
+++ b/solution.py
@@ -128,15 +128,9 @@
     left = lax.rem(z + 3, 4)
     opposite = lax.rem(z + 2, 4)
 
-    own_head = c // 2
-    is_owner = jnp.logical_and(own_head < heads, lax.rem(c, 2) == lax.rem(own_head, 2))
-
     row, lane = iotas(HEAD)
     identity = jnp.where(row == lane, 1.0, 0.0)
     which = iotas(16)[0]
-
-    def owner_of(head):
-        return 2 * head + lax.rem(head, 2)
 
     x_copy = pltpu.make_async_copy(x_hbm, x_ref, x_sem)
     x_copy.start()
@@ -277,18 +271,29 @@
     m_copy.wait()
     heard(3)
 
-    def g_copy(head):
-        owner = owner_of(head)
-        dx = lax.rem(along_x - owner // (2 * side) + side, side)
-        dy = lax.rem(along_y - lax.rem(owner // 2, side) + side, side)
-        dc = lax.rem(core + owner, 2)
-        slot = jnp.maximum((dx * side + dy) * 2 + dc - 1, 0)
+    turn = side // 2
+    own_head = lax.rem(along_x + core * turn, side) * side + lax.rem(along_y + core * turn, side)
+
+    def owner_of(head, second):
+        x = lax.rem(head // side + second * turn, side)
+        y = lax.rem(head + second * turn, side)
+        return x, y, second
+
+    def is_owner(head, second):
+        x, y, owner_core = owner_of(head, second)
+        return jnp.logical_and(jnp.logical_and(along_x == x, along_y == y), core == owner_core)
+
+    def g_copy(head, second):
+        x, y, owner_core = owner_of(head, second)
+        dx = lax.rem(along_x - x + side, side)
+        dy = lax.rem(along_y - y + side, side)
+        slot = jnp.maximum((dx * side + dy) * 2 + lax.rem(core + owner_core, 2) - 1, 0)
         return pltpu.make_async_remote_copy(
             src_ref=gsend.at[head],
             dst_ref=grecv.at[slot],
-            send_sem=gsend_sem.at[head],
+            send_sem=gsend_sem.at[head, second],
             recv_sem=grecv_sem.at[slot],
-            device_id={"cols": owner},
+            device_id={"cols": (x * side + y) * 2 + owner_core},
             device_id_type=MESH,
         )
 
@@ -315,18 +320,26 @@
                 done.append(head)
         for head in done:
 
-            @pl.when(c != owner_of(head))
-            def _():
-                g_copy(head).start()
+            for second in range(2):
+
+                @pl.when(jnp.logical_not(is_owner(head, second)))
+                def _():
+                    g_copy(head, second).start()
 
         return carry
 
     lax.fori_loop(0, chunks, finish, 0)
 
-    others = sorted(
-        ((dx, dy, dc) for dx in range(side) for dy in range(side) for dc in range(2) if dx + dy + dc),
-        key=lambda d: (min(d[0], side - d[0]) + min(d[1], side - d[1]), d[2]),
-    )
+    def far(d):
+        return min(d[0], side - d[0]) + min(d[1], side - d[1])
+
+    everyone = [(dx, dy, dc) for dx in range(side) for dy in range(side) for dc in range(2)]
+    others = sorted(everyone[1:], key=lambda d: (far(d), d[2]))
+    served = []
+    for d in others:
+        there = ((d[0] + turn) % side, (d[1] + turn) % side, d[2])
+        if far(d) < far(there) or (far(d) == far(there) and there not in served):
+            served.append(d)
 
     def f_copy(step):
         return pltpu.make_async_remote_copy(
@@ -334,12 +347,11 @@
             dst_ref=frecv.at[own_head],
             send_sem=fsend_sem.at[step],
             recv_sem=frecv_sem.at[own_head],
-            device_id={"cols": device(*others[step])},
+            device_id={"cols": device(*served[step])},
             device_id_type=MESH,
         )
 
-    @pl.when(is_owner)
-    def _():
+    def polynomial():
         def arrived(slot):
             pltpu.make_async_remote_copy(
                 src_ref=gsend.at[0],
@@ -383,15 +395,17 @@
                 rest = rest - part
         fsend[pl.ds(HALF, 16), :] = pieces.astype(BF16)
 
-        for step in reversed(range(cols - 1)):
+        for step in reversed(range(len(served))):
             f_copy(step).start()
         frecv[own_head] = fsend[...]
+
+    polynomial()
 
     def apply(k, carry):
         members = [half * half_heads + k * per_chunk + j for half in range(2) for j in range(per_chunk)]
         for head in members:
 
-            @pl.when(c != owner_of(head))
+            @pl.when(head != own_head)
             def _():
                 pltpu.make_async_remote_copy(
                     src_ref=fsend,
@@ -422,19 +436,19 @@
     lax.fori_loop(0, chunks, z_drain, 0)
 
     def g_drain(head, carry):
-        @pl.when(c != owner_of(head))
-        def _():
-            g_copy(head).wait_send()
+        for second in range(2):
+
+            @pl.when(jnp.logical_not(is_owner(head, second)))
+            def _():
+                g_copy(head, second).wait_send()
 
         return carry
 
     lax.fori_loop(0, heads, g_drain, 0)
     lax.fori_loop(0, chunks - 1, apply, 0)
 
-    @pl.when(is_owner)
-    def _():
-        for step in range(cols - 1):
-            f_copy(step).wait_send()
+    for step in range(len(served)):
+        f_copy(step).wait_send()
 
     apply(chunks - 1, 0)
 
@@ -477,7 +491,7 @@
             pltpu.SemaphoreType.DMA((16,)),
             pltpu.SemaphoreType.DMA((6, chunks)),
             pltpu.SemaphoreType.DMA((6, chunks)),
-            pltpu.SemaphoreType.DMA((heads,)),
+            pltpu.SemaphoreType.DMA((heads, 2)),
             pltpu.SemaphoreType.DMA((cols - 1,)),
             pltpu.SemaphoreType.DMA((cols,)),
             pltpu.SemaphoreType.DMA((heads,)),

time: 44.8 us -> 48.6 us (1.085)
  Pallas kernels: 44 us -> 47.8 us
    pallas_call x1, Pallas kernels: 42.7 us -> 46.4 us  [shards(): pl.pallas_call(functools.partial(kernel, dims), out_shape=(out, out), in_...]
where the time goes in v6:
time: 48.6 us; the launch traced here: 48.4 us
  Pallas kernels  47.8 us (98%)
  between operations  0.64 us (1%)
    pallas_call x1, Pallas kernels, shards(): pl.pallas_call(functools.partial(kernel, dims), out_shape=(out, out), in_...  46.4 us
    pallas_call x1, Pallas kernels, shards(): pl.pallas_call(write_out, out_shape=(jax.ShapeDtypeStruct((rows, HEAD), F...  1.33 us

profile of v6, /device:TPU:1, one launch (start us, length us, event | category | flops | bytes accessed | tf_op | source)
XLA Modules:
  0.0 48.4 jit_solution(13130615145414962707)
XLA Ops:
  0.6 46.4 %shard_map.50 = (f32[2048,128]{1,0:T(8,128)S(1)}, f32[2048,128]{1,0:T(8,128)S(1)}) custom-call(bf16[1024,128]{1,0:T(8,128)(2,1)} %x_hbm.1, bf16[1024,8192]{1,0:T(8,128)(2,1)} %q_hbm.1, f32[2048,128]{1,0:T(8,128)} %m_hbm.1), custom_call_target="tpu_custom_call" | custom-call | tf_op jit(solution)/shard_map/pallas_call | solution.py:472
  47.1 1.3 %shard_map.51 = (f32[2048,128]{1,0:T(8,128)}, f32[2048,128]{1,0:T(8,128)}) custom-call(f32[2048,128]{1,0:T(8,128)S(1)} %get-tuple-element.4.nm_ref, f32[2048,128]{1,0:T(8,128)S(1)} %get-tuple-element.5.up_ref), custom_call_target="tpu_custom_call" | custom-call | tf_op jit(solution)/shard_map/pallas_call | solution.py:504

commit v7 on v4

--- a/solution.py
+++ b/solution.py
@@ -130,6 +130,7 @@
 
     own_head = c // 2
     is_owner = jnp.logical_and(own_head < heads, lax.rem(c, 2) == lax.rem(own_head, 2))
+    own_group = lax.rem(own_head, half_heads) // (per_chunk * per_group)
 
     row, lane = iotas(HEAD)
     identity = jnp.where(row == lane, 1.0, 0.0)
@@ -145,12 +146,14 @@
         start = pl.multiple_of(target * rows + half * half_rows + g * wide, wide)
         return pltpu.make_async_copy(q_hbm.at[:, pl.ds(start, wide)], q_ref.at[slot], q_sem.at[slot])
 
-    blocks = [(opposite, 0, 0), (opposite, 1, 0), (opposite, 0, 1), (opposite, 1, 1)]
-    blocks += [(right, 1, 0), (left, 0, 0), (z, 0, 0), (z, 1, 0), (z, 0, 1), (z, 1, 1)]
-    blocks += [(right, 0, 0), (left, 1, 0), (right, 1, 1), (left, 0, 1), (right, 0, 1), (left, 1, 1)]
-    direct_slots = (4, 12)
-    own_slots = (6, 8)
-    sum_slots = (10, 14)
+    blocks = [(opposite, 0, 0), (opposite, 1, 0), (right, 1, 0), (left, 0, 0)]
+    blocks += [(z, 0, 0), (z, 1, 0), (right, 0, 0), (left, 1, 0)]
+    blocks += [(opposite, 0, 1), (opposite, 1, 1), (right, 1, 1), (left, 0, 1)]
+    blocks += [(z, 0, 1), (z, 1, 1), (right, 0, 1), (left, 1, 1)]
+    relay_slots = (0, 8)
+    direct_slots = (2, 10)
+    own_slots = (4, 12)
+    sum_slots = (6, 14)
     for slot in range(AHEAD):
         q_copy(slot, *blocks[slot]).start()
     m_copy = pltpu.make_async_copy(m_hbm, m_ref, m_sem)
@@ -186,7 +189,7 @@
         q_copy(slot, *blocks[slot]).wait()
         if slot + AHEAD < len(blocks):
             q_copy(slot + AHEAD, *blocks[slot + AHEAD]).start()
-        elif slot + 1 == len(blocks):
+        if slot + AHEAD == len(blocks):
             m_copy.start()
 
     def product(slot):
@@ -226,13 +229,12 @@
                 pl.semaphore_wait(barrier, len(near))
             z_copy(message, i, target).start()
     tell(0)
-    for g in range(1, groups):
-        q_wait(2 * g)
-        z_store(RELAY_A, g, product(2 * g))
-        z_start(RELAY_A, g, right)
-        q_wait(2 * g + 1)
-        z_store(RELAY_B, g, product(2 * g + 1))
-        z_start(RELAY_B, g, left)
+    def relay(g):
+        for half, (message, target) in enumerate(((RELAY_A, right), (RELAY_B, left))):
+            slot = relay_slots[g] + half
+            q_wait(slot)
+            z_store(message, g, product(slot))
+            z_start(message, g, target)
 
     def direct(g):
         slot = direct_slots[g]
@@ -259,23 +261,11 @@
         z_start(SUM_A, g, right)
         z_start(SUM_B, g, left)
 
-    heard(0)
-    tell(1)
-    direct(0)
-    heard(1)
-    tell(2)
-    for g in range(groups):
+    def own(g):
         for half in range(2):
             q_wait(own_slots[g] + half)
         for half in range(2):
             own_ref[half, g] = product(own_slots[g] + half)
-    heard(2)
-    tell(3)
-    sums(0)
-    direct(1)
-    sums(1)
-    m_copy.wait()
-    heard(3)
 
     def g_copy(head):
         owner = owner_of(head)
@@ -321,7 +311,6 @@
 
         return carry
 
-    lax.fori_loop(0, chunks, finish, 0)
 
     others = sorted(
         ((dx, dy, dc) for dx in range(side) for dy in range(side) for dc in range(2) if dx + dy + dc),
@@ -338,8 +327,7 @@
             device_id_type=MESH,
         )
 
-    @pl.when(is_owner)
-    def _():
+    def polynomial():
         def arrived(slot):
             pltpu.make_async_remote_copy(
                 src_ref=gsend.at[0],
@@ -386,6 +374,26 @@
         for step in reversed(range(cols - 1)):
             f_copy(step).start()
         frecv[own_head] = fsend[...]
+
+    direct(0)
+    heard(0)
+    tell(1)
+    own(0)
+    heard(1)
+    tell(2)
+    sums(0)
+    heard(2)
+    tell(3)
+    relay(1)
+    direct(1)
+    own(1)
+    m_copy.wait()
+    heard(3)
+    lax.fori_loop(0, per_group, finish, 0)
+    sums(1)
+    pl.when(jnp.logical_and(is_owner, own_group == 0))(polynomial)
+    lax.fori_loop(per_group, chunks, finish, 0)
+    pl.when(jnp.logical_and(is_owner, own_group == 1))(polynomial)
 
     def apply(k, carry):
         members = [half * half_heads + k * per_chunk + j for half in range(2) for j in range(per_chunk)]

time: 44.8 us -> 49 us (1.094)
  Pallas kernels: 44 us -> 48.2 us
    pallas_call x1, Pallas kernels: 42.7 us -> 46.9 us  [shards(): pl.pallas_call(functools.partial(kernel, dims), out_shape=(out, out), in_...]
where the time goes in v7:
time: 49 us; the launch traced here: 48.9 us
  Pallas kernels  48.2 us (98%)
  between operations  0.64 us (1%)
    pallas_call x1, Pallas kernels, shards(): pl.pallas_call(functools.partial(kernel, dims), out_shape=(out, out), in_...  46.9 us
    pallas_call x1, Pallas kernels, shards(): pl.pallas_call(write_out, out_shape=(jax.ShapeDtypeStruct((rows, HEAD), F...  1.33 us

profile of v7, /device:TPU:1, one launch (start us, length us, event | category | flops | bytes accessed | tf_op | source)
XLA Modules:
  0.0 48.9 jit_solution(594647114533867343)
XLA Ops:
  0.6 46.9 %shard_map.50 = (f32[2048,128]{1,0:T(8,128)S(1)}, f32[2048,128]{1,0:T(8,128)S(1)}) custom-call(bf16[1024,128]{1,0:T(8,128)(2,1)} %x_hbm.1, bf16[1024,8192]{1,0:T(8,128)(2,1)} %q_hbm.1, f32[2048,128]{1,0:T(8,128)} %m_hbm.1), custom_call_target="tpu_custom_call" | custom-call | tf_op jit(solution)/shard_map/pallas_call | solution.py:466
  47.5 1.3 %shard_map.51 = (f32[2048,128]{1,0:T(8,128)}, f32[2048,128]{1,0:T(8,128)}) custom-call(f32[2048,128]{1,0:T(8,128)S(1)} %get-tuple-element.4.nm_ref, f32[2048,128]{1,0:T(8,128)S(1)} %get-tuple-element.5.up_ref), custom_call_target="tpu_custom_call" | custom-call | tf_op jit(solution)/shard_map/pallas_call | solution.py:498

commit v8 on v4

--- a/solution.py
+++ b/solution.py
@@ -186,7 +186,7 @@
         q_copy(slot, *blocks[slot]).wait()
         if slot + AHEAD < len(blocks):
             q_copy(slot + AHEAD, *blocks[slot + AHEAD]).start()
-        elif slot + 1 == len(blocks):
+        if slot + AHEAD == len(blocks):
             m_copy.start()
 
     def product(slot):
@@ -273,7 +273,6 @@
     tell(3)
     sums(0)
     direct(1)
-    sums(1)
     m_copy.wait()
     heard(3)
 
@@ -321,7 +320,9 @@
 
         return carry
 
-    lax.fori_loop(0, chunks, finish, 0)
+    finish(0, 0)
+    sums(1)
+    lax.fori_loop(1, chunks, finish, 0)
 
     others = sorted(
         ((dx, dy, dc) for dx in range(side) for dy in range(side) for dc in range(2) if dx + dy + dc),

time: 44.8 us -> 44.6 us (level)
  no operation moved by 1% of the time
where the time goes in v8:
time: 44.6 us; the launch traced here: 44.5 us
  Pallas kernels  43.8 us (98%)
  between operations  0.64 us (1%)
    pallas_call x1, Pallas kernels, shards(): pl.pallas_call(functools.partial(kernel, dims), out_shape=(out, out), in_...  42.5 us
    pallas_call x1, Pallas kernels, shards(): pl.pallas_call(write_out, out_shape=(jax.ShapeDtypeStruct((rows, HEAD), F...  1.33 us

profile of v8, /device:TPU:1, one launch (start us, length us, event | category | flops | bytes accessed | tf_op | source)
XLA Modules:
  0.0 44.5 jit_solution(14788302500311806333)
XLA Ops:
  0.6 42.5 %shard_map.50 = (f32[2048,128]{1,0:T(8,128)S(1)}, f32[2048,128]{1,0:T(8,128)S(1)}) custom-call(bf16[1024,128]{1,0:T(8,128)(2,1)} %x_hbm.1, bf16[1024,8192]{1,0:T(8,128)(2,1)} %q_hbm.1, f32[2048,128]{1,0:T(8,128)} %m_hbm.1), custom_call_target="tpu_custom_call" | custom-call | tf_op jit(solution)/shard_map/pallas_call | solution.py:459
  43.1 1.3 %shard_map.51 = (f32[2048,128]{1,0:T(8,128)}, f32[2048,128]{1,0:T(8,128)}) custom-call(f32[2048,128]{1,0:T(8,128)S(1)} %get-tuple-element.4.nm_ref, f32[2048,128]{1,0:T(8,128)S(1)} %get-tuple-element.5.up_ref), custom_call_target="tpu_custom_call" | custom-call | tf_op jit(solution)/shard_map/pallas_call | solution.py:491
